TPU v7x, 32 devices: a whole 2x2x4 slice. The times are simulated.
32 devices in a mesh: survey: 2 (over x), gx: 16 (over z, y, core).
Axes of the slice: x: 2, y: 2, z: 4, core: 2. Of those that a mesh axis runs over, the one named last changes fastest.
Arguments:
- courant: float32 [256, 256, 256], P('gx', 'survey'), parts along dimension 1, may hold values from 0.06 to 0.24
- sketches: bfloat16 [4, 4, 256, 128, 256], P('survey', None, 'gx'), parts along dimension 0, may hold values from -6 to 6
- probes: float32 [4, 8, 4], P('survey'), parts along dimension 0, may hold values from -6 to 6
- source_spot: int32 [4, 3], P('survey'), parts along dimension 0, may hold values from 0 to 255, as said below
- wavelet: float32 [4, 8], P('survey'), parts along dimension 0, may hold values from -48 to 48
- adjoint_before: float32 [4, 256, 128, 256], P('survey', 'gx'), parts along dimension 0, may hold values from -2 to 2
- adjoint_start: float32 [4, 256, 128, 256], P('survey', 'gx'), parts along dimension 0, may hold values from -2 to 2
Outputs:
- imaging: float32 [256, 256, 256], P('gx', 'survey'), parts along dimension 1
- adjoint_end: float32 [4, 256, 128, 256], P('survey', 'gx'), parts along dimension 0
There are 2 independent parts, one for each index of `survey`. A program takes and returns all parts, laid end to end along the dimension named above; each array names one. Nothing has to cross between parts.
Inputs may be any that keep to these rules, and one draw needn't show every extreme that they name: `source_spot`: column 0 lies below 256, column 1 below 128, column 2 below 256.
All inputs are finite; a program needn't handle non-finite values.
Results may differ from a plain program's by a relative error of at most 0.0003.
Values sent between devices are 32-bit elements; how exact they have to be, the bound alone decides.
No kernel may reach another device: no remote copies, remote signals or barrier semaphores. Data moves between devices by JAX's collectives and lax.ppermute only.
A program may use at most 192 MiB of HBM per device.

v0:
```python
import jax
import jax.numpy as jnp
from jax import lax
from jax.sharding import PartitionSpec as P

STEPS = 8
FRAMES = 4


def padded_2(cells, sides, width):
    for axis, dim in sides:
        count = lax.axis_size(axis)
        ends = count - 1
        head = lax.slice_in_dim(cells, 0, width, axis=dim)
        tail = lax.slice_in_dim(cells, cells.shape[dim] - width, cells.shape[dim], axis=dim)
        cells = jnp.concatenate(
            [
                lax.ppermute(tail, axis, [(i, (i + 1) % count) for i in range(ends)]),
                cells,
                lax.ppermute(head, axis, [((i + 1) % count, i) for i in range(ends)]),
            ],
            axis=dim,
        )
    return cells


def laplace_center(padded):
    center = padded[:, 2:-2]
    total = (
        -(padded[:, :-4] + padded[:, 4:]) / 12.0
        + (padded[:, 1:-3] + padded[:, 3:-1]) * (4.0 / 3.0)
        - 2.5 * center
    )
    wide_y = jnp.pad(center, ((0, 0), (0, 0), (2, 2), (0, 0)))
    total = (
        total
        - (wide_y[:, :, :-4] + wide_y[:, :, 4:]) / 12.0
        + (wide_y[:, :, 1:-3] + wide_y[:, :, 3:-1]) * (4.0 / 3.0)
        - 2.5 * center
    )
    wide_z = jnp.pad(center, ((0, 0), (0, 0), (0, 0), (2, 2)))
    total = (
        total
        - (wide_z[:, :, :, :-4] + wide_z[:, :, :, 4:]) / 12.0
        + (wide_z[:, :, :, 1:-3] + wide_z[:, :, :, 3:-1]) * (4.0 / 3.0)
        - 2.5 * center
    )
    return total


def inject(spots, amplitude, coords, breadth, height):
    plane = (coords[None, :] == spots[:, 0:1]).astype(jnp.float32)
    row_hit = (jnp.arange(breadth, dtype=jnp.int32)[None, :] == spots[:, 1:2]).astype(jnp.float32)
    col_hit = (jnp.arange(height, dtype=jnp.int32)[None, :] == spots[:, 2:3]).astype(jnp.float32)
    return (
        amplitude[:, None, None, None]
        * plane[:, :, None, None]
        * row_hit[:, None, :, None]
        * col_hit[:, None, None, :]
    )


def accumulate(image, lighting, current, sketches, probes, instant):
    weighted = jnp.zeros_like(current)
    for sketch_index in range(FRAMES):
        weighted = weighted + probes[:, instant, sketch_index][:, None, None, None] * sketches[
            :, sketch_index
        ].astype(jnp.float32)
    image = image + jnp.sum(weighted * current, axis=0)
    lighting = lighting + jnp.sum(current * current, axis=0)
    return (image, lighting)


def per_device(courant, sketches, probes, source_spot, wavelet, adjoint_before, adjoint_start):
    shots, planes, breadth, height = adjoint_start.shape
    offset = lax.axis_index("gx") * planes
    own_coords = offset + jnp.arange(planes, dtype=jnp.int32)
    previous = adjoint_before
    current = adjoint_start
    image = jnp.zeros((planes, breadth, height), jnp.float32)
    lighting = jnp.zeros((planes, breadth, height), jnp.float32)
    for instant in range(STEPS):
        padded = padded_2(current, (("gx", 1),), 2)
        advanced = (
            2.0 * current
            - previous
            + courant[None] * laplace_center(padded)
            + inject(source_spot, wavelet[:, instant], own_coords, breadth, height)
        )
        previous = current
        current = advanced
        image, lighting = accumulate(image, lighting, current, sketches, probes, instant)
    largest = lax.pmax(jnp.max(lighting), "gx")
    return (image / (lighting + 0.1 * largest), current)


def solution(mesh):
    placed = (
        P("gx", "survey", None),
        P("survey", None, "gx", None, None),
        P("survey", None, None),
        P("survey", None),
        P("survey", None),
        P("survey", "gx", None, None),
        P("survey", "gx", None, None),
    )
    return jax.shard_map(
        per_device,
        mesh=mesh,
        in_specs=placed,
        out_specs=(P("gx", "survey", None), P("survey", "gx", None, None)),
        check_vma=False,
    )
```

profile of v0, /device:TPU:0, one launch (start us, length us, event | category | flops | bytes accessed | tf_op | source)
XLA Modules:
  0.0 372.2 jit_solution(7047546794184077522)
XLA Ops:
  14.1 8.6 %fusion.119 = f32[2,16,128,256]{3,2,1,0:T(8,128)S(1)} fusion(f32[2,16,128,256]{3,2,1,0:T(8,128)S(1)} %copy-done.5, f32[2,18,128,256]{3,2,1,0:T(8,128)S(1)} %constant_dynamic-update-slice_fusion.2, f32[2,18,128,256]{3,2,1,0:T(8,128)} %copy-done.6, f32[2,16,128,256]{3,2,1,0:T(8,128)} %param.12, f32[2,256]{1,0:T(2,128)S(1)} %compare_convert_fusion, ...), kind=kLoop, calls=%fused_computation.211 | loop fusion | flops 29360128 | bytes 31475712 | tf_op jit(solution)/shard_map/add | solution.py:85
  22.8 12.3 %collective-permute-start.2 = (f32[2,2,128,256]{3,2,1,0:T(8,128)S(1)}, f32[2,2,128,256]{3,2,1,0:T(8,128)S(1)}, u32[]{:S(2)}, u32[]{:S(2)}) collective-permute-start(f32[2,2,128,256]{3,2,1,0:T(8,128)S(1)} %get-tuple-element.79), channel_id=1, source_target_pairs={{0,1},{1,2},{2,3},{3,4},{4,5},{5,6},{6,7},{7,8},{8,9},{9,10},{10,1... | collective-permute-start | bytes 1572872 | tf_op jit(solution)/shard_map/ppermute | solution.py:18
  36.6 4.3 %collective-permute-done.3 = f32[2,2,128,256]{3,2,1,0:T(8,128)S(1)} collective-permute-done((f32[2,2,128,256]{3,2,1,0:T(8,128)S(1)}, f32[2,2,128,256]{3,2,1,0:T(8,128)S(1)}, u32[]{:S(2)}, u32[]{:S(2)}) %collective-permute-start.3) | collective-permute-done | bytes 524320 | tf_op jit(solution)/shard_map/ppermute | solution.py:20
  40.9 10.1 %fusion.110 = f32[2,16,128,256]{3,2,1,0:T(8,128)S(1)} fusion(f32[2,16,128,256]{3,2,1,0:T(8,128)S(1)} %fusion.119, f32[2,2,128,256]{3,2,1,0:T(8,128)S(1)} %collective-permute-done.3, f32[2,2,128,256]{3,2,1,0:T(8,128)S(1)} %collective-permute-done.2, f32[2,16,128,256]{3,2,1,0:T(8,128)} %param.13, f32[2,16,128]{2,1,0:T(8,128)S(1)} %get-tuple-element.86, ...), kind=kLoop, calls=%fused_computation.202 | loop fusion | flops 33554432 | bytes 15747072 | tf_op jit(solution)/shard_map/add | solution.py:85
  51.1 10.4 %collective-permute-start.4 = (f32[2,2,128,256]{3,2,1,0:T(8,128)S(1)}, f32[2,2,128,256]{3,2,1,0:T(8,128)S(1)}, u32[]{:S(2)}, u32[]{:S(2)}) collective-permute-start(f32[2,2,128,256]{3,2,1,0:T(8,128)S(1)} %get-tuple-element.77), channel_id=1, source_target_pairs={{0,1},{1,2},{2,3},{3,4},{4,5},{5,6},{6,7},{7,8},{8,9},{9,10},{10,1... | collective-permute-start | bytes 1572872 | tf_op jit(solution)/shard_map/ppermute | solution.py:18
  63.0 4.3 %collective-permute-done.5 = f32[2,2,128,256]{3,2,1,0:T(8,128)S(1)} collective-permute-done((f32[2,2,128,256]{3,2,1,0:T(8,128)S(1)}, f32[2,2,128,256]{3,2,1,0:T(8,128)S(1)}, u32[]{:S(2)}, u32[]{:S(2)}) %collective-permute-start.5) | collective-permute-done | bytes 524320 | tf_op jit(solution)/shard_map/ppermute | solution.py:20
  67.2 22.8 %fusion.94 = f32[2,16,128,256]{3,2,1,0:T(8,128)S(1)} fusion(f32[2,16,128,256]{3,2,1,0:T(8,128)} %copy-done.4, f32[2,2,128,256]{3,2,1,0:T(8,128)S(1)} %collective-permute-done.5, f32[2,2,128,256]{3,2,1,0:T(8,128)S(1)} %collective-permute-done.4, f32[2,16,128,256]{3,2,1,0:T(8,128)S(1)} %fusion.119, f32[2,16,128]{2,1,0:T(8,128)S(1)} %get-tuple-element.87, ...), kind=kLoop, calls=%fused_computation.186 | loop fusion | flops 33554432 | bytes 15747072 | tf_op jit(solution)/shard_map/add | solution.py:85
  90.1 10.4 %collective-permute-start.6 = (f32[2,2,128,256]{3,2,1,0:T(8,128)S(1)}, f32[2,2,128,256]{3,2,1,0:T(8,128)S(1)}, u32[]{:S(2)}, u32[]{:S(2)}) collective-permute-start(f32[2,2,128,256]{3,2,1,0:T(8,128)S(1)} %get-tuple-element.75), channel_id=1, source_target_pairs={{0,1},{1,2},{2,3},{3,4},{4,5},{5,6},{6,7},{7,8},{8,9},{9,10},{10,1... | collective-permute-start | bytes 1572872 | tf_op jit(solution)/shard_map/ppermute | solution.py:18
  102.0 4.3 %collective-permute-done.7 = f32[2,2,128,256]{3,2,1,0:T(8,128)S(1)} collective-permute-done((f32[2,2,128,256]{3,2,1,0:T(8,128)S(1)}, f32[2,2,128,256]{3,2,1,0:T(8,128)S(1)}, u32[]{:S(2)}, u32[]{:S(2)}) %collective-permute-start.7) | collective-permute-done | bytes 524320 | tf_op jit(solution)/shard_map/ppermute | solution.py:20
  106.2 10.1 %fusion.78 = f32[2,16,128,256]{3,2,1,0:T(8,128)S(1)} fusion(f32[2,16,128,256]{3,2,1,0:T(8,128)S(1)} %fusion.94, f32[2,2,128,256]{3,2,1,0:T(8,128)S(1)} %collective-permute-done.7, f32[2,2,128,256]{3,2,1,0:T(8,128)S(1)} %collective-permute-done.6, f32[2,16,128,256]{3,2,1,0:T(8,128)} %copy-done.4, f32[2,16,128]{2,1,0:T(8,128)S(1)} %get-tuple-element.88, ...), kind=kLoop, calls=%fused_computation.170 | loop fusion | flops 33554432 | bytes 15747072 | tf_op jit(solution)/shard_map/add | solution.py:85
  118.4 10.4 %collective-permute-start.8 = (f32[2,2,128,256]{3,2,1,0:T(8,128)S(1)}, f32[2,2,128,256]{3,2,1,0:T(8,128)S(1)}, u32[]{:S(2)}, u32[]{:S(2)}) collective-permute-start(f32[2,2,128,256]{3,2,1,0:T(8,128)S(1)} %get-tuple-element.73), channel_id=1, source_target_pairs={{0,1},{1,2},{2,3},{3,4},{4,5},{5,6},{6,7},{7,8},{8,9},{9,10},{10,1... | collective-permute-start | bytes 1572872 | tf_op jit(solution)/shard_map/ppermute | solution.py:18
  130.7 3.8 %collective-permute-done.9 = f32[2,2,128,256]{3,2,1,0:T(8,128)S(1)} collective-permute-done((f32[2,2,128,256]{3,2,1,0:T(8,128)S(1)}, f32[2,2,128,256]{3,2,1,0:T(8,128)S(1)}, u32[]{:S(2)}, u32[]{:S(2)}) %collective-permute-start.9) | collective-permute-done | bytes 524320 | tf_op jit(solution)/shard_map/ppermute | solution.py:20
  134.5 32.3 %fusion.159 = (f32[16,128,256]{2,1,0:T(8,128)}, f32[16,128,256]{2,1,0:T(8,128)}, f32[16,128,256]{2,1,0:T(8,128)}, f32[16,128,256]{2,1,0:T(8,128)}, f32[2,16,128,256]{3,2,1,0:T(8,128)}) fusion(f32[2,16,128,256]{3,2,1,0:T(8,128)} %copy-done.4, f32[2]{0:T(128)S(1)} %get-tuple-element.42, f32[2]{0:T(128)S(1)} %get-tuple-element.43, f32[2]{0:T(128)S(1)} %get-tuple-element.37, ...), kind=kLoop, calls=%fused_computation.251 | loop fusion | flops 58720256 | bytes 36718656 | tf_op jit(solution)/shard_map/reduce_sum | solution.py:69
  168.1 10.4 %collective-permute-start.10 = (f32[2,2,128,256]{3,2,1,0:T(8,128)S(1)}, f32[2,2,128,256]{3,2,1,0:T(8,128)S(1)}, u32[]{:S(2)}, u32[]{:S(2)}) collective-permute-start(f32[2,2,128,256]{3,2,1,0:T(8,128)S(1)} %get-tuple-element.71), channel_id=1, source_target_pairs={{0,1},{1,2},{2,3},{3,4},{4,5},{5,6},{6,7},{7,8},{8,9},{9,10},{10,1... | collective-permute-start | bytes 1572872 | tf_op jit(solution)/shard_map/ppermute | solution.py:18
  180.0 4.3 %collective-permute-done.11 = f32[2,2,128,256]{3,2,1,0:T(8,128)S(1)} collective-permute-done((f32[2,2,128,256]{3,2,1,0:T(8,128)S(1)}, f32[2,2,128,256]{3,2,1,0:T(8,128)S(1)}, u32[]{:S(2)}, u32[]{:S(2)}) %collective-permute-start.11) | collective-permute-done | bytes 524320 | tf_op jit(solution)/shard_map/ppermute | solution.py:20
  184.2 33.3 %fusion.154 = (f32[16,128,256]{2,1,0:T(8,128)}, f32[16,128,256]{2,1,0:T(8,128)}, f32[16,128,256]{2,1,0:T(8,128)}, f32[16,128,256]{2,1,0:T(8,128)}, f32[2,16,128,256]{3,2,1,0:T(8,128)}) fusion(f32[2,16,128,256]{3,2,1,0:T(8,128)} %copy-done.2, f32[2]{0:T(128)S(1)} %get-tuple-element.44, f32[2]{0:T(128)S(1)} %get-tuple-element.45, f32[2]{0:T(128)S(1)} %get-tuple-element.46, ...), kind=kLoop, calls=%fused_computation.246 | loop fusion | flops 58720256 | bytes 36718656 | tf_op jit(solution)/shard_map/reduce_sum | solution.py:69
  218.8 10.2 %collective-permute-start.12 = (f32[2,2,128,256]{3,2,1,0:T(8,128)S(1)}, f32[2,2,128,256]{3,2,1,0:T(8,128)S(1)}, u32[]{:S(2)}, u32[]{:S(2)}) collective-permute-start(f32[2,2,128,256]{3,2,1,0:T(8,128)S(1)} %get-tuple-element.69), channel_id=1, source_target_pairs={{0,1},{1,2},{2,3},{3,4},{4,5},{5,6},{6,7},{7,8},{8,9},{9,10},{10,1... | collective-permute-start | bytes 1572872 | tf_op jit(solution)/shard_map/ppermute | solution.py:18
  230.5 4.2 %collective-permute-done.13 = f32[2,2,128,256]{3,2,1,0:T(8,128)S(1)} collective-permute-done((f32[2,2,128,256]{3,2,1,0:T(8,128)S(1)}, f32[2,2,128,256]{3,2,1,0:T(8,128)S(1)}, u32[]{:S(2)}, u32[]{:S(2)}) %collective-permute-start.13) | collective-permute-done | bytes 524320 | tf_op jit(solution)/shard_map/ppermute | solution.py:20
  234.7 32.3 %fusion.164 = (f32[16,128,256]{2,1,0:T(8,128)}, f32[16,128,256]{2,1,0:T(8,128)}, f32[16,128,256]{2,1,0:T(8,128)}, f32[16,128,256]{2,1,0:T(8,128)}, f32[2,16,128,256]{3,2,1,0:T(8,128)}) fusion(f32[2,16,128,256]{3,2,1,0:T(8,128)} %copy-done.3, f32[2]{0:T(128)S(1)} %get-tuple-element.38, f32[2]{0:T(128)S(1)} %get-tuple-element.39, f32[2]{0:T(128)S(1)} %get-tuple-element.40, ...), kind=kLoop, calls=%fused_computation.256 | loop fusion | flops 58720256 | bytes 36718656 | tf_op jit(solution)/shard_map/reduce_sum | solution.py:69
  268.3 9.1 %collective-permute-start.14 = (f32[2,2,128,256]{3,2,1,0:T(8,128)S(1)}, f32[2,2,128,256]{3,2,1,0:T(8,128)S(1)}, u32[]{:S(2)}, u32[]{:S(2)}) collective-permute-start(f32[2,2,128,256]{3,2,1,0:T(8,128)S(1)} %get-tuple-element.67), channel_id=1, source_target_pairs={{0,1},{1,2},{2,3},{3,4},{4,5},{5,6},{6,7},{7,8},{8,9},{9,10},{10,1... | collective-permute-start | bytes 1572872 | tf_op jit(solution)/shard_map/ppermute | solution.py:18
  282.5 32.8 %fusion.169 = (f32[16,128,256]{2,1,0:T(8,128)}, f32[16,128,256]{2,1,0:T(8,128)}, f32[16,128,256]{2,1,0:T(8,128)}, f32[16,128,256]{2,1,0:T(8,128)}, f32[2,16,128,256]{3,2,1,0:T(8,128)}) fusion(f32[2,16,128,256]{3,2,1,0:T(8,128)} %copy-done.1, f32[2]{0:T(128)S(1)} %get-tuple-element.33, f32[2]{0:T(128)S(1)} %get-tuple-element.34, f32[2]{0:T(128)S(1)} %get-tuple-element.35, ...), kind=kLoop, calls=%fused_computation.261 | loop fusion | flops 58720256 | bytes 36718656 | tf_op jit(solution)/shard_map/reduce_sum | solution.py:69
  315.3 9.7 %fusion.226 = (f32[]{:T(128)}, f32[16,128,256]{2,1,0:T(8,128)}) fusion(f32[16,128,256]{2,1,0:T(8,128)} %get-tuple-element.10, f32[16,128,256]{2,1,0:T(8,128)} %get-tuple-element.11, f32[16,128,256]{2,1,0:T(8,128)} %get-tuple-element.12, f32[16,128,256]{2,1,0:T(8,128)} %get-tuple-element.13, f32[16,128,256]{2,1,0:T(8,128)} %get-tuple-element.17, ...), kind=kLoop, calls=%fused_computation.425 | loop fusion | flops 4194303 | bytes 18874372 | tf_op jit(solution)/shard_map/reduce_max | solution.py:93
  325.0 37.4 %pmax.7 = f32[]{:T(128)} all-reduce(f32[]{:T(128)} %get-tuple-element.61), channel_id=1, replica_groups=mesh['survey'=2,'gx'=16] {'gx'}, use_global_device_ids=true, to_apply=%region_17.18 | all-reduce | flops 1 | bytes 8 | tf_op jit(solution)/shard_map/pmax | solution.py:93
  363.0 9.2 %add_divide_fusion = f32[16,128,256]{2,1,0:T(8,128)} fusion(f32[16,128,256]{2,1,0:T(8,128)} %get-tuple-element.62, f32[16,128,256]{2,1,0:T(8,128)} %get-tuple-element.9, f32[16,128,256]{2,1,0:T(8,128)} %get-tuple-element.7, f32[16,128,256]{2,1,0:T(8,128)} %get-tuple-element.5, f32[16,128,256]{2,1,0:T(8,128)} %get-tuple-element.3, ...), kind=kLoop, calls=%fused_computation.357 | loop fusion | flops 4718592 | bytes 20971524 | tf_op jit(solution)/shard_map/div | solution.py:94
  (57 shorter events, 33.8 us)
Async XLA Ops:
  1.9 6.4 %collective-permute-start = (f32[2,2,128,256]{3,2,1,0:T(8,128)S(1)}, f32[2,2,128,256]{3,2,1,0:T(8,128)S(1)}, u32[]{:S(2)}, u32[]{:S(2)}) collective-permute-start(f32[2,2,128,256]{3,2,1,0:T(8,128)S(1)} %get-tuple-element.83), channel_id=1, source_target_pairs={{0,1},{1,2},{2,3},{3,4},{4,5},{5,6},{6,7},{7,8},{8,9},{9,10},{10,1... | collective-permute-start | bytes 1572872 | tf_op jit(solution)/shard_map/ppermute | solution.py:18
  4.4 7.7 %collective-permute-start.1 = (f32[2,2,128,256]{3,2,1,0:T(8,128)S(1)}, f32[2,2,128,256]{3,2,1,0:T(8,128)S(1)}, u32[]{:S(2)}, u32[]{:S(2)}) collective-permute-start(f32[2,2,128,256]{3,2,1,0:T(8,128)S(1)} %get-tuple-element.84), channel_id=1, source_target_pairs={{1,0},{2,1},{3,2},{4,3},{5,4},{6,5},{7,6},{8,7},{9,8},{10,9},{11,1... | collective-permute-start | bytes 1572872 | tf_op jit(solution)/shard_map/ppermute | solution.py:20
  8.3 5.8 %copy-start = (f32[16,128,256]{2,1,0:T(8,128)S(1)}, f32[16,128,256]{2,1,0:T(8,128)}, u32[]{:S(2)}) copy-start(f32[16,128,256]{2,1,0:T(8,128)} %param.7) | copy-start | bytes 6291460
  8.4 5.8 %copy-start.5 = (f32[2,16,128,256]{3,2,1,0:T(8,128)S(1)}, f32[2,16,128,256]{3,2,1,0:T(8,128)}, u32[]{:S(2)}) copy-start(f32[2,16,128,256]{3,2,1,0:T(8,128)} %param.13) | copy-start | bytes 12582916
  12.0 2.1 copy-start.6
  22.7 44.5 %copy-start.2 = (f32[2,16,128,256]{3,2,1,0:T(8,128)}, f32[2,16,128,256]{3,2,1,0:T(8,128)S(1)}, u32[]{:S(2)}) copy-start(f32[2,16,128,256]{3,2,1,0:T(8,128)S(1)} %fusion.119) | copy-start | bytes 12582916
  22.8 13.8 %collective-permute-start.2 = (f32[2,2,128,256]{3,2,1,0:T(8,128)S(1)}, f32[2,2,128,256]{3,2,1,0:T(8,128)S(1)}, u32[]{:S(2)}, u32[]{:S(2)}) collective-permute-start(f32[2,2,128,256]{3,2,1,0:T(8,128)S(1)} %get-tuple-element.79), channel_id=1, source_target_pairs={{0,1},{1,2},{2,3},{3,4},{4,5},{5,6},{6,7},{7,8},{8,9},{9,10},{10,1... | collective-permute-start | bytes 1572872 | tf_op jit(solution)/shard_map/ppermute | solution.py:18
  35.1 5.8 %collective-permute-start.3 = (f32[2,2,128,256]{3,2,1,0:T(8,128)S(1)}, f32[2,2,128,256]{3,2,1,0:T(8,128)S(1)}, u32[]{:S(2)}, u32[]{:S(2)}) collective-permute-start(f32[2,2,128,256]{3,2,1,0:T(8,128)S(1)} %get-tuple-element.80), channel_id=1, source_target_pairs={{1,0},{2,1},{3,2},{4,3},{5,4},{6,5},{7,6},{8,7},{9,8},{10,9},{11,1... | collective-permute-start | bytes 1572872 | tf_op jit(solution)/shard_map/ppermute | solution.py:20
  51.0 16.2 %copy-start.4 = (f32[2,16,128,256]{3,2,1,0:T(8,128)}, f32[2,16,128,256]{3,2,1,0:T(8,128)S(1)}, u32[]{:S(2)}) copy-start(f32[2,16,128,256]{3,2,1,0:T(8,128)S(1)} %fusion.110) | copy-start | bytes 12582916
  51.1 11.8 %collective-permute-start.4 = (f32[2,2,128,256]{3,2,1,0:T(8,128)S(1)}, f32[2,2,128,256]{3,2,1,0:T(8,128)S(1)}, u32[]{:S(2)}, u32[]{:S(2)}) collective-permute-start(f32[2,2,128,256]{3,2,1,0:T(8,128)S(1)} %get-tuple-element.77), channel_id=1, source_target_pairs={{0,1},{1,2},{2,3},{3,4},{4,5},{5,6},{6,7},{7,8},{8,9},{9,10},{10,1... | collective-permute-start | bytes 1572872 | tf_op jit(solution)/shard_map/ppermute | solution.py:18
  61.5 5.8 %collective-permute-start.5 = (f32[2,2,128,256]{3,2,1,0:T(8,128)S(1)}, f32[2,2,128,256]{3,2,1,0:T(8,128)S(1)}, u32[]{:S(2)}, u32[]{:S(2)}) collective-permute-start(f32[2,2,128,256]{3,2,1,0:T(8,128)S(1)} %get-tuple-element.78), channel_id=1, source_target_pairs={{1,0},{2,1},{3,2},{4,3},{5,4},{6,5},{7,6},{8,7},{9,8},{10,9},{11,1... | collective-permute-start | bytes 1572872 | tf_op jit(solution)/shard_map/ppermute | solution.py:20
  90.0 26.4 %copy-start.3 = (f32[2,16,128,256]{3,2,1,0:T(8,128)}, f32[2,16,128,256]{3,2,1,0:T(8,128)S(1)}, u32[]{:S(2)}) copy-start(f32[2,16,128,256]{3,2,1,0:T(8,128)S(1)} %fusion.94) | copy-start | bytes 12582916
  90.1 11.9 %collective-permute-start.6 = (f32[2,2,128,256]{3,2,1,0:T(8,128)S(1)}, f32[2,2,128,256]{3,2,1,0:T(8,128)S(1)}, u32[]{:S(2)}, u32[]{:S(2)}) collective-permute-start(f32[2,2,128,256]{3,2,1,0:T(8,128)S(1)} %get-tuple-element.75), channel_id=1, source_target_pairs={{0,1},{1,2},{2,3},{3,4},{4,5},{5,6},{6,7},{7,8},{8,9},{9,10},{10,1... | collective-permute-start | bytes 1572872 | tf_op jit(solution)/shard_map/ppermute | solution.py:18
  100.5 5.8 %collective-permute-start.7 = (f32[2,2,128,256]{3,2,1,0:T(8,128)S(1)}, f32[2,2,128,256]{3,2,1,0:T(8,128)S(1)}, u32[]{:S(2)}, u32[]{:S(2)}) collective-permute-start(f32[2,2,128,256]{3,2,1,0:T(8,128)S(1)} %get-tuple-element.76), channel_id=1, source_target_pairs={{1,0},{2,1},{3,2},{4,3},{5,4},{6,5},{7,6},{8,7},{9,8},{10,9},{11,1... | collective-permute-start | bytes 1572872 | tf_op jit(solution)/shard_map/ppermute | solution.py:20
  106.2 24.0 %copy-start.8 = (f32[2,8,4]{1,2,0:T(4,128)S(1)}, f32[2,8,4]{1,2,0:T(4,128)}, u32[]{:S(2)}) copy-start(f32[2,8,4]{1,2,0:T(4,128)} %param.9) | copy-start | bytes 772
  118.4 12.3 %collective-permute-start.8 = (f32[2,2,128,256]{3,2,1,0:T(8,128)S(1)}, f32[2,2,128,256]{3,2,1,0:T(8,128)S(1)}, u32[]{:S(2)}, u32[]{:S(2)}) collective-permute-start(f32[2,2,128,256]{3,2,1,0:T(8,128)S(1)} %get-tuple-element.73), channel_id=1, source_target_pairs={{0,1},{1,2},{2,3},{3,4},{4,5},{5,6},{6,7},{7,8},{8,9},{9,10},{10,1... | collective-permute-start | bytes 1572872 | tf_op jit(solution)/shard_map/ppermute | solution.py:18
  128.8 5.8 %collective-permute-start.9 = (f32[2,2,128,256]{3,2,1,0:T(8,128)S(1)}, f32[2,2,128,256]{3,2,1,0:T(8,128)S(1)}, u32[]{:S(2)}, u32[]{:S(2)}) collective-permute-start(f32[2,2,128,256]{3,2,1,0:T(8,128)S(1)} %get-tuple-element.74), channel_id=1, source_target_pairs={{1,0},{2,1},{3,2},{4,3},{5,4},{6,5},{7,6},{8,7},{9,8},{10,9},{11,1... | collective-permute-start | bytes 1572872 | tf_op jit(solution)/shard_map/ppermute | solution.py:20
  168.1 11.8 %collective-permute-start.10 = (f32[2,2,128,256]{3,2,1,0:T(8,128)S(1)}, f32[2,2,128,256]{3,2,1,0:T(8,128)S(1)}, u32[]{:S(2)}, u32[]{:S(2)}) collective-permute-start(f32[2,2,128,256]{3,2,1,0:T(8,128)S(1)} %get-tuple-element.71), channel_id=1, source_target_pairs={{0,1},{1,2},{2,3},{3,4},{4,5},{5,6},{6,7},{7,8},{8,9},{9,10},{10,1... | collective-permute-start | bytes 1572872 | tf_op jit(solution)/shard_map/ppermute | solution.py:18
  178.5 5.8 %collective-permute-start.11 = (f32[2,2,128,256]{3,2,1,0:T(8,128)S(1)}, f32[2,2,128,256]{3,2,1,0:T(8,128)S(1)}, u32[]{:S(2)}, u32[]{:S(2)}) collective-permute-start(f32[2,2,128,256]{3,2,1,0:T(8,128)S(1)} %get-tuple-element.72), channel_id=1, source_target_pairs={{1,0},{2,1},{3,2},{4,3},{5,4},{6,5},{7,6},{8,7},{9,8},{10,9},{11,1... | collective-permute-start | bytes 1572872 | tf_op jit(solution)/shard_map/ppermute | solution.py:20
  218.8 11.7 %collective-permute-start.12 = (f32[2,2,128,256]{3,2,1,0:T(8,128)S(1)}, f32[2,2,128,256]{3,2,1,0:T(8,128)S(1)}, u32[]{:S(2)}, u32[]{:S(2)}) collective-permute-start(f32[2,2,128,256]{3,2,1,0:T(8,128)S(1)} %get-tuple-element.69), channel_id=1, source_target_pairs={{0,1},{1,2},{2,3},{3,4},{4,5},{5,6},{6,7},{7,8},{8,9},{9,10},{10,1... | collective-permute-start | bytes 1572872 | tf_op jit(solution)/shard_map/ppermute | solution.py:18
  229.0 5.8 %collective-permute-start.13 = (f32[2,2,128,256]{3,2,1,0:T(8,128)S(1)}, f32[2,2,128,256]{3,2,1,0:T(8,128)S(1)}, u32[]{:S(2)}, u32[]{:S(2)}) collective-permute-start(f32[2,2,128,256]{3,2,1,0:T(8,128)S(1)} %get-tuple-element.70), channel_id=1, source_target_pairs={{1,0},{2,1},{3,2},{4,3},{5,4},{6,5},{7,6},{8,7},{9,8},{10,9},{11,1... | collective-permute-start | bytes 1572872 | tf_op jit(solution)/shard_map/ppermute | solution.py:20
  268.3 10.6 %collective-permute-start.14 = (f32[2,2,128,256]{3,2,1,0:T(8,128)S(1)}, f32[2,2,128,256]{3,2,1,0:T(8,128)S(1)}, u32[]{:S(2)}, u32[]{:S(2)}) collective-permute-start(f32[2,2,128,256]{3,2,1,0:T(8,128)S(1)} %get-tuple-element.67), channel_id=1, source_target_pairs={{0,1},{1,2},{2,3},{3,4},{4,5},{5,6},{6,7},{7,8},{8,9},{9,10},{10,1... | collective-permute-start | bytes 1572872 | tf_op jit(solution)/shard_map/ppermute | solution.py:18
  277.4 5.1 %collective-permute-start.15 = (f32[2,2,128,256]{3,2,1,0:T(8,128)S(1)}, f32[2,2,128,256]{3,2,1,0:T(8,128)S(1)}, u32[]{:S(2)}, u32[]{:S(2)}) collective-permute-start(f32[2,2,128,256]{3,2,1,0:T(8,128)S(1)} %get-tuple-element.68), channel_id=1, source_target_pairs={{1,0},{2,1},{3,2},{4,3},{5,4},{6,5},{7,6},{8,7},{9,8},{10,9},{11,1... | collective-permute-start | bytes 1572872 | tf_op jit(solution)/shard_map/ppermute | solution.py:20
  315.3 47.8 %copy-start.7 = (f32[16,128,256]{2,1,0:T(8,128)S(1)}, f32[16,128,256]{2,1,0:T(8,128)}, u32[]{:S(2)}) copy-start(f32[16,128,256]{2,1,0:T(8,128)} %get-tuple-element.2) | copy-start | bytes 6291460
  (1 other events, 1.9 us)
where the time goes:
time: 373 us; the launch traced here: 372 us
  other arithmetic  201 us (54%)
  starting transfers between devices  86.2 us (23%)
  blocking collectives  37.4 us (10%)
  waiting for transfers between devices  29.7 us (8%)
  local copies, waits for them, and re-layouts  15.8 us (4%)
    reduce_sum x4, other arithmetic, accumulate(): image = image + jnp.sum(weighted * current, axis=0)  131 us
    ppermute x8, starting transfers between devices, padded_2(): lax.ppermute(tail, axis, [(i, (i + 1) % count) for i in range(ends)])  75.5 us
    add x4, other arithmetic, per_device(): 2.0 * current - previous + courant[None] * laplace_center(padded)  51.6 us
    pmax x1, blocking collectives, per_device(): largest = lax.pmax(jnp.max(lighting), 'gx')  37.4 us
    ppermute x8, waiting for transfers between devices, padded_2(): lax.ppermute(head, axis, [((i + 1) % count, i) for i in range(ends)])  28.8 us
    ppermute x8, starting transfers between devices, padded_2(): lax.ppermute(head, axis, [((i + 1) % count, i) for i in range(ends)])  10.7 us
    reduce_max x1, other arithmetic, per_device(): largest = lax.pmax(jnp.max(lighting), 'gx')  9.68 us
    div x1, other arithmetic, per_device(): return (image / (lighting + 0.1 * largest), current)  9.15 us
  transfers between devices with their start and end apart: 16, of which 12 were waited for; matrix products, arithmetic and copies ran while one was open for 2% of the time, Pallas kernels for 0%

commit v1 on v0

v1 whole, which is shorter than its diff:
```python
import functools

import jax
import jax.numpy as jnp
from jax import lax
from jax.experimental import pallas as pl
from jax.experimental.pallas import tpu as pltpu
from jax.sharding import PartitionSpec as P

F32 = jnp.float32
BF16 = jnp.bfloat16
VMEM = pl.BlockSpec(memory_space=pltpu.VMEM)
SMEM = pl.BlockSpec(memory_space=pltpu.SMEM)
ANY = pl.BlockSpec(memory_space=pl.ANY)
EDGE = 2


def held(*dims):
    return pltpu.VMEM(dims, F32)


def in_hbm(array):
    return pltpu.with_memory_space_constraint(array, pltpu.HBM)


def call(body, outs, ins, aliases=None, scratch=(), flops=0, moved=0, limit=6 << 20):
    return pl.pallas_call(
        body,
        out_shape=outs,
        in_specs=ins,
        out_specs=jax.tree.map(lambda _: VMEM, outs),
        scratch_shapes=scratch,
        input_output_aliases=aliases or {},
        compiler_params=pltpu.CompilerParams(vmem_limit_bytes=limit),
        cost_estimate=pl.CostEstimate(flops=flops, bytes_accessed=moved, transcendentals=0),
    )


def orientation(planes, far):
    odd = lax.rem(lax.axis_index("gx"), 2)
    sign = 2 * odd - 1
    base = (1 - odd) * (planes - 1)
    return (base + sign * (planes - 1), -sign) if far else (base, sign)


def pack_body(far, shots, planes, start, *refs):
    outs, sems = refs[:-1], refs[-1]
    base, sign = orientation(planes, far)
    started = []
    for s in range(shots):
        for d in range(EDGE):
            target = outs[s].at[d] if far else outs[0].at[s * EDGE + d]
            copy = pltpu.make_async_copy(start.at[s, base + sign * d], target, sems.at[s * EDGE + d])
            copy.start()
            started.append(copy)
    for copy in started:
        copy.wait()


def dot(a, b):
    return lax.dot_general(a, b, (((1,), (0,)), ((), ())), preferred_element_type=F32)


def advance(down2, down1, mid, up1, up2, last, scaled, along_z, along_y):
    high = mid.astype(BF16)
    low = (mid - high.astype(F32)).astype(BF16)
    total = dot(high, along_z) + dot(low, along_z) + dot(along_y, jnp.concatenate([high, low], axis=0))
    total = total + (16.0 * (down1 + up1) - (down2 + up2))
    return 2.0 * mid - last + scaled * total


def inject(ref, here, row, column, amount):
    @pl.when(here)
    def _():
        top = pl.multiple_of((row // 8) * 8, 8)
        tile = ref[pl.ds(top, 8), :]
        rows = lax.broadcasted_iota(jnp.int32, tile.shape, 0)
        columns = lax.broadcasted_iota(jnp.int32, tile.shape, 1)
        ref[pl.ds(top, 8), :] = tile + jnp.where((rows == row - top) & (columns == column), amount, 0.0)


def source(planes, spots, wavelet, instant, s, base, sign, target, low, high):
    plane = spots[s, 0] - lax.axis_index("gx") * planes
    own = (plane - base) * sign
    inject(
        target.at[s, jnp.clip(plane, 0, planes - 1)], (own >= low) & (own < high),
        spots[s, 1], spots[s, 2], wavelet[s, instant],
    )


def main_body(shots, planes, frames, instant, spots, wavelet, probes, field, last, courant, along_z, along_y, ghost, *refs):
    refs = list(refs)
    images = instant > 0
    adds = instant > 1
    if images:
        sketches = refs.pop(0)
    if adds:
        image_in, light_in = refs[:2]
        del refs[:2]
    ahead, send = refs[:2]
    del refs[:2]
    base, sign = orientation(planes, False)

    def at(j):
        return base + sign * j

    def now(s, j):
        return ghost[s * EDGE - 1 - j] if isinstance(j, int) and j < 0 else field[s, at(j)]

    def step(j):
        scaled = courant[at(j)] * (1.0 / 12.0)
        for s in range(shots):
            five = [now(s, j + d) for d in (-2, -1, 0, 1, 2)]
            ahead[s, at(j)] = advance(*five, last[s, at(j)], scaled, along_z[...], along_y[...])

    def body(j, carry):
        step(j)
        return carry

    for j in range(EDGE):
        step(j)
    lax.fori_loop(EDGE, planes - EDGE, body, 0, unroll=2)
    for s in range(shots):
        source(planes, spots, wavelet, instant, s, base, sign, ahead, 0, planes - EDGE)
    for s in range(shots):
        for d in range(EDGE):
            send[s * EDGE + d] = ahead[s, at(d)]
    if images:
        add_image(shots, planes, frames, (instant - 1,), (field,), probes, sketches,
                  (image_in, light_in) if adds else None, refs[0], refs[1])


def far_body(shot, planes, instant, spots, wavelet, probes, field, last, courant, along_z, along_y, ghost, partial, ahead, *refs):
    base, sign = orientation(planes, True)
    index = lax.axis_index("gx")
    inner = (index > 0) & (index < lax.axis_size("gx") - 1)

    def at(k):
        return base + sign * k

    def now(k):
        return jnp.where(inner, ghost[-1 - k], 0.0) if k < 0 else field[shot, at(k)]

    for k in range(EDGE):
        five = [now(k + d) for d in (-2, -1, 0, 1, 2)]
        ahead[shot, at(k)] = advance(
            *five, last[shot, at(k)], courant[at(k)] * (1.0 / 12.0), along_z[...], along_y[...]
        )
    source(planes, spots, wavelet, instant, shot, base, sign, ahead, 0, EDGE)
    if refs:
        for k in range(EDGE):
            refs[0][k] = ahead[shot, at(k)]


def add_image(shots, planes, frames, instants, fields, probes, sketches, before, image_out, light_out):
    breadth = image_out.shape[1]
    chunk = 16
    per = breadth // chunk

    def body(number, carry):
        p = number // per
        rows = pl.ds(pl.multiple_of((number % per) * chunk, chunk), chunk)
        image = light = None
        if before is not None:
            image, light = before[0][p, rows, :], before[1][p, rows, :]
        for s in range(shots):
            drawn = [sketches[s, k, p, rows, :].astype(F32) for k in range(frames)]
            for instant, field in zip(instants, fields):
                value = field[s, p, rows, :]
                weighted = probes[s, instant, 0] * drawn[0]
                for k in range(1, frames):
                    weighted = weighted + probes[s, instant, k] * drawn[k]
                image = weighted * value if image is None else image + weighted * value
                light = value * value if light is None else light + value * value
        image_out[p, rows, :] = image
        light_out[p, rows, :] = light
        return carry

    lax.fori_loop(0, planes * per, body, 0, unroll=2)


def last_body(shots, planes, frames, instant, probes, sketches, field, image_in, light_in, image_out, light_out, most):
    add_image(shots, planes, frames, (instant,), (field,), probes, sketches, (image_in, light_in), image_out, light_out)
    breadth, height = light_out.shape[1:]

    def highest(p):
        return jnp.max(light_out[p].reshape(breadth // 8, 8, height), axis=0)

    most[...] = lax.fori_loop(1, planes, lambda p, so_far: jnp.maximum(so_far, highest(p)), highest(0))


def divide_body(planes, image, light, most, out):
    largest = 0.1 * jnp.max(most[...])

    def body(p, carry):
        out[p] = image[p] / (light[p] + largest)
        return carry

    lax.fori_loop(0, planes, body, 0)


def per_device(courant, sketches, probes, source_spot, wavelet, adjoint_before, adjoint_start):
    shots, planes, breadth, height = adjoint_start.shape
    frames, steps = sketches.shape[1], wavelet.shape[1]
    count, areas = lax.axis_size("gx"), lax.axis_size("survey")

    def band(size, center):
        apart = jnp.abs(jnp.arange(size)[:, None] - jnp.arange(size)[None, :])
        return jnp.where(apart == 0, center, jnp.where(apart == 1, 16.0, jnp.where(apart == 2, -1.0, 0.0))).astype(BF16)

    along_z = band(height, -60.0)
    along_y = band(breadth, -30.0)
    along_y = jnp.concatenate([along_y, along_y], axis=1)

    near_pairs = [(i, i ^ 1) for i in range(count)]
    far_pairs = []
    for area in range(areas):
        for i in range(count):
            other = i + 1 if i % 2 else i - 1
            if 0 <= other < count:
                far_pairs.append((area * count + i, area * count + other))
            elif areas % 2 == 0:
                far_pairs.append((area * count + i, (area ^ 1) * count + i))
    plane_bytes = 4 * breadth * height
    whole = held(shots, planes, breadth, height)
    still = held(planes, breadth, height)
    edge = held(EDGE, breadth, height)
    both = held(shots * EDGE, breadth, height)

    def to_far(planes_out):
        return lax.ppermute(planes_out, ("survey", "gx"), far_pairs)

    def to_near(planes_out):
        return lax.ppermute(planes_out, "gx", near_pairs)

    def pack(far):
        return call(
            functools.partial(pack_body, far, shots, planes),
            (edge,) * shots if far else (both,), [ANY], scratch=[pltpu.SemaphoreType.DMA((shots * EDGE,))],
            moved=4 * shots * plane_bytes,
        )(in_hbm(adjoint_start))

    far = [to_far(part) for part in pack(True)]
    near = to_near(pack(False)[0])
    field, last = adjoint_start, adjoint_before
    images = ()
    for instant in range(steps):
        closing = instant == steps - 1
        shared = [source_spot, wavelet, probes, field, last, courant, along_z, along_y]
        specs = [SMEM] * 3 + [VMEM] * 5
        extra, extra_specs, aliases, outs = [], [], {}, (whole, both)
        if instant > 0:
            extra, extra_specs = [sketches, *images], [VMEM] * (1 + len(images))
            outs = outs + (still, still)
        if images:
            at = len(shared) + 2
            aliases = {at: 2, at + 1: 3}
        ahead, near_sent, *images = call(
            functools.partial(main_body, shots, planes, frames, instant), outs,
            specs + [VMEM] + extra_specs, aliases=aliases,
            flops=2 * planes * shots * breadth * height * 512, moved=8 * planes * shots * plane_bytes,
        )(*shared, near, *extra)
        if not closing:
            near = to_near(near_sent)
        for shot in range(shots):
            at = len(shared) + 1
            ahead, *sent = call(
                functools.partial(far_body, shot, planes, instant),
                (whole,) if closing else (whole, edge), specs + [VMEM] * 2, aliases={at: 0},
                flops=4 * breadth * height * 512, moved=16 * plane_bytes,
            )(*shared, far[shot], ahead)
            if not closing:
                far[shot] = to_far(sent[0])
        field, last = ahead, field
    image, light, most = call(
        functools.partial(last_body, shots, planes, frames, steps - 1),
        (still, still, held(8, height)), [SMEM] + [VMEM] * 4, aliases={3: 0, 4: 1},
        moved=8 * planes * shots * plane_bytes,
    )(probes, sketches, field, *images)
    reach = 1
    while reach < count:
        most = jnp.maximum(most, lax.ppermute(most, "gx", [(i, i ^ reach) for i in range(count)]))
        reach *= 2
    result = call(
        functools.partial(divide_body, planes), jax.ShapeDtypeStruct((planes, breadth, height), F32), [VMEM] * 3,
        moved=3 * planes * plane_bytes,
    )(image, light, most)
    return result, field


def solution(mesh):
    placed = (
        P("gx", "survey", None),
        P("survey", None, "gx", None, None),
        P("survey", None, None),
        P("survey", None),
        P("survey", None),
        P("survey", "gx", None, None),
        P("survey", "gx", None, None),
    )
    return jax.shard_map(
        per_device,
        mesh=mesh,
        in_specs=placed,
        out_specs=(P("gx", "survey", None), P("survey", "gx", None, None)),
        check_vma=False,
    )
```

time: 373 us -> 202 us (0.54)
  other arithmetic: 201 us -> 0.11 us
  Pallas kernels: 0 us -> 76.6 us
  blocking collectives: 37.4 us -> 0 us
  starting transfers between devices: 86.2 us -> 65.8 us
  waiting for transfers between devices: 29.7 us -> 49 us
  local copies, waits for them, and re-layouts: 15.8 us -> 8.94 us
    reduce_sum x4 -> x0, other arithmetic: 131 us -> none  [accumulate(): image = image + jnp.sum(weighted * current, axis=0)]
    pallas_call x0 -> x28, Pallas kernels: none -> 76.6 us  [the longest x8 52.4 us: per_device(): call(functools.partial(main_body, shots, planes, frames, instant), outs,...]
    add x5 -> x0, other arithmetic: 51.6 us -> none  [the longest x4 51.6 us: per_device(): 2.0 * current - previous + courant[None] * laplace_center(padded)]
    pmax x1 -> x0, blocking collectives: 37.4 us -> none  [per_device(): largest = lax.pmax(jnp.max(lighting), 'gx')]
    ppermute x16 -> x28, starting transfers between devices: 86.2 us -> 65.8 us  [the longest x8 31.7 us: to_near(): return lax.ppermute(planes_out, 'gx', near_pairs)]
    ppermute x16 -> x28, waiting for transfers between devices: 29.7 us -> 49 us  [the longest x16 41.4 us: to_far(): return lax.ppermute(planes_out, ('survey', 'gx'), far_pairs)]
    reduce_max x1 -> x0, other arithmetic: 9.68 us -> none  [per_device(): largest = lax.pmax(jnp.max(lighting), 'gx')]
    div x1 -> x0, other arithmetic: 9.15 us -> none  [per_device(): return (image / (lighting + 0.1 * largest), current)]
  transfers between devices with their start and end apart: 16 -> 28, of which waited for: 12 -> 18; matrix products, arithmetic and copies ran while one was open for 2% -> 1% of each run, Pallas kernels for 0% -> 12%
where the time goes in v1:
time: 202 us; the launch traced here: 201 us
  Pallas kernels  76.6 us (38%)
  starting transfers between devices  65.8 us (33%)
  waiting for transfers between devices  49 us (24%)
  local copies, waits for them, and re-layouts  8.94 us (4%)
    pallas_call x8, Pallas kernels, per_device(): call(functools.partial(main_body, shots, planes, frames, instant), outs,...  52.4 us
    ppermute x16, waiting for transfers between devices, to_far(): return lax.ppermute(planes_out, ('survey', 'gx'), far_pairs)  41.4 us
    ppermute x8, starting transfers between devices, to_near(): return lax.ppermute(planes_out, 'gx', near_pairs)  31.7 us
    ppermute x16, starting transfers between devices, to_far(): return lax.ppermute(planes_out, ('survey', 'gx'), far_pairs)  17.9 us
    ppermute x4, starting transfers between devices, per_device(): lax.ppermute(most, 'gx', [(i, i ^ reach) for i in range(count)])  16.2 us
    pallas_call x16, Pallas kernels, per_device(): call(functools.partial(far_body, shot, planes, instant), (whole,) if clos...  16 us
    unnamed x20, local copies, waits for them, and re-layouts  8.94 us
    ppermute x4, waiting for transfers between devices, per_device(): lax.ppermute(most, 'gx', [(i, i ^ reach) for i in range(count)])  6.31 us
  transfers between devices with their start and end apart: 28, of which 18 were waited for; matrix products, arithmetic and copies ran while one was open for 1% of the time, Pallas kernels for 12%

profile of v1, /device:TPU:0, one launch (start us, length us, event | category | flops | bytes accessed | tf_op | source)
XLA Modules:
  0.0 201.5 jit_solution(7623482084234605796)
XLA Ops:
  8.4 3.8 %shard_map.88 = (f32[2,16,128,256]{3,2,1,0:T(8,128)S(1)}, f32[4,128,256]{2,1,0:T(8,128)S(1)}) custom-call(s32[2,3]{1,0:T(2,128)S(1)} %copy-done.4, f32[2,8]{1,0:T(2,128)S(1)} %copy-done.5, f32[2,8,4]{2,1,0:T(8,128)S(1)} %copy.63.probes, f32[2,16,128,256]{3,2,1,0:T(8,128)S(1)} %copy-done.1, f32[2,16,128,256]{3,2,1,0:T(8,128)S(1)} %copy-done.3, ...), custom_call_target="tpu_custom_call" | custom-call | flops 1073741824 | bytes 33554432 | tf_op jit(solution)/shard_map/pallas_call | solution.py:258
  16.7 4.3 %collective-permute-done.1.ghost = f32[2,128,256]{2,1,0:T(8,128)S(1)} collective-permute-done((f32[2,128,256]{2,1,0:T(8,128)S(1)}, f32[2,128,256]{2,1,0:T(8,128)S(1)}, u32[]{:S(2)}, u32[]{:S(2)}) %collective-permute-start.1) | collective-permute-done | bytes 262176 | tf_op jit(solution)/shard_map/ppermute | solution.py:231
  27.3 6.8 %shard_map.91 = (f32[2,16,128,256]{3,2,1,0:T(8,128)S(1)}, f32[4,128,256]{2,1,0:T(8,128)S(1)}, f32[16,128,256]{2,1,0:T(8,128)S(1)}, f32[16,128,256]{2,1,0:T(8,128)S(1)}) custom-call(s32[2,3]{1,0:T(2,128)S(1)} %copy-done.4, f32[2,8]{1,0:T(2,128)S(1)} %copy-done.5, f32[2,8,4]{2,1,0:T(8,128)S(1)} %copy.63.probes, ...), custom_call_target="tpu_custom_call" | custom-call | flops 1073741824 | bytes 33554432 | tf_op jit(solution)/shard_map/pallas_call | solution.py:258
  34.1 4.8 %collective-permute-start.8 = (f32[4,128,256]{2,1,0:T(8,128)S(1)}, f32[4,128,256]{2,1,0:T(8,128)S(1)}, u32[]{:S(2)}, u32[]{:S(2)}) collective-permute-start(f32[4,128,256]{2,1,0:T(8,128)S(1)} %get-tuple-element.77), channel_id=1, source_target_pairs={{0,1},{1,0},{2,3},{3,2},{4,5},{5,4},{6,7},{7,6},{8,9},{9,8},{10,11... | collective-permute-start | bytes 1572872 | tf_op jit(solution)/shard_map/ppermute | solution.py:234
  40.9 4.3 %collective-permute-done.4.ghost = f32[2,128,256]{2,1,0:T(8,128)S(1)} collective-permute-done((f32[2,128,256]{2,1,0:T(8,128)S(1)}, f32[2,128,256]{2,1,0:T(8,128)S(1)}, u32[]{:S(2)}, u32[]{:S(2)}) %collective-permute-start.4) | collective-permute-done | bytes 262176 | tf_op jit(solution)/shard_map/ppermute | solution.py:231
  49.1 6.8 %shard_map.94 = (f32[2,16,128,256]{3,2,1,0:T(8,128)S(1)}, f32[4,128,256]{2,1,0:T(8,128)S(1)}, f32[16,128,256]{2,1,0:T(8,128)S(1)}, f32[16,128,256]{2,1,0:T(8,128)S(1)}) custom-call(s32[2,3]{1,0:T(2,128)S(1)} %copy-done.4, f32[2,8]{1,0:T(2,128)S(1)} %copy-done.5, f32[2,8,4]{2,1,0:T(8,128)S(1)} %copy.63.probes, ...), custom_call_target="tpu_custom_call", output_to_operand_aliasing={{2}: (10, {}), {3}: (11, {})} | custom-call | flops 1073741824 | bytes 33554432 | tf_op jit(solution)/shard_map/pallas_call | solution.py:258
  55.9 5.2 %collective-permute-start.11 = (f32[4,128,256]{2,1,0:T(8,128)S(1)}, f32[4,128,256]{2,1,0:T(8,128)S(1)}, u32[]{:S(2)}, u32[]{:S(2)}) collective-permute-start(f32[4,128,256]{2,1,0:T(8,128)S(1)} %get-tuple-element.85), channel_id=1, source_target_pairs={{0,1},{1,0},{2,3},{3,2},{4,5},{5,4},{6,7},{7,6},{8,9},{9,8},{10,11... | collective-permute-start | bytes 1572872 | tf_op jit(solution)/shard_map/ppermute | solution.py:234
  63.1 4.3 %collective-permute-done.7.ghost = f32[2,128,256]{2,1,0:T(8,128)S(1)} collective-permute-done((f32[2,128,256]{2,1,0:T(8,128)S(1)}, f32[2,128,256]{2,1,0:T(8,128)S(1)}, u32[]{:S(2)}, u32[]{:S(2)}) %collective-permute-start.7) | collective-permute-done | bytes 262176 | tf_op jit(solution)/shard_map/ppermute | solution.py:231
  71.3 6.8 %shard_map.97 = (f32[2,16,128,256]{3,2,1,0:T(8,128)S(1)}, f32[4,128,256]{2,1,0:T(8,128)S(1)}, f32[16,128,256]{2,1,0:T(8,128)S(1)}, f32[16,128,256]{2,1,0:T(8,128)S(1)}) custom-call(s32[2,3]{1,0:T(2,128)S(1)} %copy-done.4, f32[2,8]{1,0:T(2,128)S(1)} %copy-done.5, f32[2,8,4]{2,1,0:T(8,128)S(1)} %copy.63.probes, ...), custom_call_target="tpu_custom_call", output_to_operand_aliasing={{2}: (10, {}), {3}: (11, {})} | custom-call | flops 1073741824 | bytes 33554432 | tf_op jit(solution)/shard_map/pallas_call | solution.py:258
  78.1 5.2 %collective-permute-start.14 = (f32[4,128,256]{2,1,0:T(8,128)S(1)}, f32[4,128,256]{2,1,0:T(8,128)S(1)}, u32[]{:S(2)}, u32[]{:S(2)}) collective-permute-start(f32[4,128,256]{2,1,0:T(8,128)S(1)} %get-tuple-element.93), channel_id=1, source_target_pairs={{0,1},{1,0},{2,3},{3,2},{4,5},{5,4},{6,7},{7,6},{8,9},{9,8},{10,11... | collective-permute-start | bytes 1572872 | tf_op jit(solution)/shard_map/ppermute | solution.py:234
  85.3 4.3 %collective-permute-done.10.ghost = f32[2,128,256]{2,1,0:T(8,128)S(1)} collective-permute-done((f32[2,128,256]{2,1,0:T(8,128)S(1)}, f32[2,128,256]{2,1,0:T(8,128)S(1)}, u32[]{:S(2)}, u32[]{:S(2)}) %collective-permute-start.10) | collective-permute-done | bytes 262176 | tf_op jit(solution)/shard_map/ppermute | solution.py:231
  93.5 6.8 %shard_map.100 = (f32[2,16,128,256]{3,2,1,0:T(8,128)S(1)}, f32[4,128,256]{2,1,0:T(8,128)S(1)}, f32[16,128,256]{2,1,0:T(8,128)S(1)}, f32[16,128,256]{2,1,0:T(8,128)S(1)}) custom-call(s32[2,3]{1,0:T(2,128)S(1)} %copy-done.4, f32[2,8]{1,0:T(2,128)S(1)} %copy-done.5, f32[2,8,4]{2,1,0:T(8,128)S(1)} %copy.63.probes, ...), custom_call_target="tpu_custom_call", output_to_operand_aliasing={{2}: (10, {}), {3}: (11, {})} | custom-call | flops 1073741824 | bytes 33554432 | tf_op jit(solution)/shard_map/pallas_call | solution.py:258
  100.3 5.2 %collective-permute-start.17 = (f32[4,128,256]{2,1,0:T(8,128)S(1)}, f32[4,128,256]{2,1,0:T(8,128)S(1)}, u32[]{:S(2)}, u32[]{:S(2)}) collective-permute-start(f32[4,128,256]{2,1,0:T(8,128)S(1)} %get-tuple-element.101), channel_id=1, source_target_pairs={{0,1},{1,0},{2,3},{3,2},{4,5},{5,4},{6,7},{7,6},{8,9},{9,8},{10,11... | collective-permute-start | bytes 1572872 | tf_op jit(solution)/shard_map/ppermute | solution.py:234
  107.5 4.3 %collective-permute-done.13.ghost = f32[2,128,256]{2,1,0:T(8,128)S(1)} collective-permute-done((f32[2,128,256]{2,1,0:T(8,128)S(1)}, f32[2,128,256]{2,1,0:T(8,128)S(1)}, u32[]{:S(2)}, u32[]{:S(2)}) %collective-permute-start.13) | collective-permute-done | bytes 262176 | tf_op jit(solution)/shard_map/ppermute | solution.py:231
  115.7 6.8 %shard_map.103 = (f32[2,16,128,256]{3,2,1,0:T(8,128)S(1)}, f32[4,128,256]{2,1,0:T(8,128)S(1)}, f32[16,128,256]{2,1,0:T(8,128)S(1)}, f32[16,128,256]{2,1,0:T(8,128)S(1)}) custom-call(s32[2,3]{1,0:T(2,128)S(1)} %copy-done.4, f32[2,8]{1,0:T(2,128)S(1)} %copy-done.5, f32[2,8,4]{2,1,0:T(8,128)S(1)} %copy.63.probes, ...), custom_call_target="tpu_custom_call", output_to_operand_aliasing={{2}: (10, {}), {3}: (11, {})} | custom-call | flops 1073741824 | bytes 33554432 | tf_op jit(solution)/shard_map/pallas_call | solution.py:258
  122.5 5.2 %collective-permute-start.20 = (f32[4,128,256]{2,1,0:T(8,128)S(1)}, f32[4,128,256]{2,1,0:T(8,128)S(1)}, u32[]{:S(2)}, u32[]{:S(2)}) collective-permute-start(f32[4,128,256]{2,1,0:T(8,128)S(1)} %get-tuple-element.109), channel_id=1, source_target_pairs={{0,1},{1,0},{2,3},{3,2},{4,5},{5,4},{6,7},{7,6},{8,9},{9,8},{10,11... | collective-permute-start | bytes 1572872 | tf_op jit(solution)/shard_map/ppermute | solution.py:234
  129.7 4.3 %collective-permute-done.16.ghost = f32[2,128,256]{2,1,0:T(8,128)S(1)} collective-permute-done((f32[2,128,256]{2,1,0:T(8,128)S(1)}, f32[2,128,256]{2,1,0:T(8,128)S(1)}, u32[]{:S(2)}, u32[]{:S(2)}) %collective-permute-start.16) | collective-permute-done | bytes 262176 | tf_op jit(solution)/shard_map/ppermute | solution.py:231
  137.9 7.0 %shard_map.106 = (f32[2,16,128,256]{3,2,1,0:T(8,128)S(1)}, f32[4,128,256]{2,1,0:T(8,128)S(1)}, f32[16,128,256]{2,1,0:T(8,128)S(1)}, f32[16,128,256]{2,1,0:T(8,128)S(1)}) custom-call(s32[2,3]{1,0:T(2,128)S(1)} %copy-done.4, f32[2,8]{1,0:T(2,128)S(1)} %copy-done.5, f32[2,8,4]{2,1,0:T(8,128)S(1)} %copy.63.probes, ...), custom_call_target="tpu_custom_call", output_to_operand_aliasing={{2}: (10, {}), {3}: (11, {})} | custom-call | flops 1073741824 | bytes 33554432 | tf_op jit(solution)/shard_map/pallas_call | solution.py:258
  144.9 5.2 %collective-permute-start.23 = (f32[4,128,256]{2,1,0:T(8,128)S(1)}, f32[4,128,256]{2,1,0:T(8,128)S(1)}, u32[]{:S(2)}, u32[]{:S(2)}) collective-permute-start(f32[4,128,256]{2,1,0:T(8,128)S(1)} %get-tuple-element.117), channel_id=1, source_target_pairs={{0,1},{1,0},{2,3},{3,2},{4,5},{5,4},{6,7},{7,6},{8,9},{9,8},{10,11... | collective-permute-start | bytes 1572872 | tf_op jit(solution)/shard_map/ppermute | solution.py:234
  152.1 4.3 %collective-permute-done.19.ghost = f32[2,128,256]{2,1,0:T(8,128)S(1)} collective-permute-done((f32[2,128,256]{2,1,0:T(8,128)S(1)}, f32[2,128,256]{2,1,0:T(8,128)S(1)}, u32[]{:S(2)}, u32[]{:S(2)}) %collective-permute-start.19) | collective-permute-done | bytes 262176 | tf_op jit(solution)/shard_map/ppermute | solution.py:231
  161.8 7.6 %shard_map.109 = (f32[2,16,128,256]{3,2,1,0:T(8,128)S(1)}, f32[4,128,256]{2,1,0:T(8,128)}, f32[16,128,256]{2,1,0:T(8,128)S(1)}, f32[16,128,256]{2,1,0:T(8,128)S(1)}) custom-call(s32[2,3]{1,0:T(2,128)S(1)} %copy-done.4, f32[2,8]{1,0:T(2,128)S(1)} %copy-done.5, f32[2,8,4]{2,1,0:T(8,128)S(1)} %copy.63.probes, ...), custom_call_target="tpu_custom_call", output_to_operand_aliasing={{2}: (10, {}), {3}: (11, {})} | custom-call | flops 1073741824 | bytes 33554432 | tf_op jit(solution)/shard_map/pallas_call | solution.py:258
  171.4 3.6 %shard_map.112 = (f32[16,128,256]{2,1,0:T(8,128)S(1)}, f32[16,128,256]{2,1,0:T(8,128)S(1)}, f32[8,256]{1,0:T(8,128)S(1)}) custom-call(f32[2,8,4]{2,1,0:T(8,128)S(1)} %copy.63.probes, bf16[2,4,16,128,256]{4,3,2,1,0:T(8,128)(2,1)S(1)} %bitcast.1, f32[2,16,128,256]{3,2,1,0:T(8,128)S(1)} %shard_map.111.field, ...), custom_call_target="tpu_custom_call", output_to_operand_aliasing={{0}: (3, {}), {1}: (4, {})} | custom-call | bytes 33554432 | tf_op jit(solution)/shard_map/pallas_call | solution.py:275
  175.0 11.8 %collective-permute-start.24 = (f32[8,256]{1,0:T(8,128)S(1)}, f32[8,256]{1,0:T(8,128)S(1)}, u32[]{:S(2)}, u32[]{:S(2)}) collective-permute-start(f32[8,256]{1,0:T(8,128)S(1)} %get-tuple-element.125), channel_id=1, source_target_pairs={{0,1},{1,0},{2,3},{3,2},{4,5},{5,4},{6,7},{7,6},{8,9},{9,8},{10,11... | collective-permute-start | bytes 24584 | tf_op jit(solution)/shard_map/ppermute | solution.py:282
  188.0 3.4 %collective-permute-done.25 = f32[8,256]{1,0:T(8,128)S(1)} collective-permute-done((f32[8,256]{1,0:T(8,128)S(1)}, f32[8,256]{1,0:T(8,128)S(1)}, u32[]{:S(2)}, u32[]{:S(2)}) %collective-permute-start.25) | collective-permute-done | bytes 8224 | tf_op jit(solution)/shard_map/ppermute | solution.py:282
  (88 shorter events, 68.2 us)
Async XLA Ops:
  12.3 12.6 %collective-permute-start.5 = (f32[4,128,256]{2,1,0:T(8,128)S(1)}, f32[4,128,256]{2,1,0:T(8,128)S(1)}, u32[]{:S(2)}, u32[]{:S(2)}) collective-permute-start(f32[4,128,256]{2,1,0:T(8,128)S(1)} %get-tuple-element.71), channel_id=1, source_target_pairs={{0,1},{1,0},{2,3},{3,2},{4,5},{5,4},{6,7},{7,6},{8,9},{9,8},{10,11... | collective-permute-start | bytes 1572872 | tf_op jit(solution)/shard_map/ppermute | solution.py:234
  14.1 7.0 %collective-permute-start.1 = (f32[2,128,256]{2,1,0:T(8,128)S(1)}, f32[2,128,256]{2,1,0:T(8,128)S(1)}, u32[]{:S(2)}, u32[]{:S(2)}) collective-permute-start(f32[2,128,256]{2,1,0:T(8,128)S(1)} %get-tuple-element.65), channel_id=1, source_target_pairs={{0,16},{1,2},{2,1},{3,4},{4,3},{5,6},{6,5},{7,8},{8,7},{9,10},{10,... | collective-permute-start | bytes 786440 | tf_op jit(solution)/shard_map/ppermute | solution.py:231
  16.7 7.2 %collective-permute-start = (f32[2,128,256]{2,1,0:T(8,128)S(1)}, f32[2,128,256]{2,1,0:T(8,128)S(1)}, u32[]{:S(2)}, u32[]{:S(2)}) collective-permute-start(f32[2,128,256]{2,1,0:T(8,128)S(1)} %get-tuple-element.64), channel_id=1, source_target_pairs={{0,16},{1,2},{2,1},{3,4},{4,3},{5,6},{6,5},{7,8},{8,7},{9,10},{10,... | collective-permute-start | bytes 786440 | tf_op jit(solution)/shard_map/ppermute | solution.py:231
  34.1 15.0 %collective-permute-start.8 = (f32[4,128,256]{2,1,0:T(8,128)S(1)}, f32[4,128,256]{2,1,0:T(8,128)S(1)}, u32[]{:S(2)}, u32[]{:S(2)}) collective-permute-start(f32[4,128,256]{2,1,0:T(8,128)S(1)} %get-tuple-element.77), channel_id=1, source_target_pairs={{0,1},{1,0},{2,3},{3,2},{4,5},{5,4},{6,7},{7,6},{8,9},{9,8},{10,11... | collective-permute-start | bytes 1572872 | tf_op jit(solution)/shard_map/ppermute | solution.py:234
  38.9 6.4 %collective-permute-start.4 = (f32[2,128,256]{2,1,0:T(8,128)S(1)}, f32[2,128,256]{2,1,0:T(8,128)S(1)}, u32[]{:S(2)}, u32[]{:S(2)}) collective-permute-start(f32[2,128,256]{2,1,0:T(8,128)S(1)} %get-tuple-element.70), channel_id=1, source_target_pairs={{0,16},{1,2},{2,1},{3,4},{4,3},{5,6},{6,5},{7,8},{8,7},{9,10},{10,... | collective-permute-start | bytes 786440 | tf_op jit(solution)/shard_map/ppermute | solution.py:231
  40.3 7.7 %collective-permute-start.3 = (f32[2,128,256]{2,1,0:T(8,128)S(1)}, f32[2,128,256]{2,1,0:T(8,128)S(1)}, u32[]{:S(2)}, u32[]{:S(2)}) collective-permute-start(f32[2,128,256]{2,1,0:T(8,128)S(1)} %get-tuple-element.69), channel_id=1, source_target_pairs={{0,16},{1,2},{2,1},{3,4},{4,3},{5,6},{6,5},{7,8},{8,7},{9,10},{10,... | collective-permute-start | bytes 786440 | tf_op jit(solution)/shard_map/ppermute | solution.py:231
  55.9 15.4 %collective-permute-start.11 = (f32[4,128,256]{2,1,0:T(8,128)S(1)}, f32[4,128,256]{2,1,0:T(8,128)S(1)}, u32[]{:S(2)}, u32[]{:S(2)}) collective-permute-start(f32[4,128,256]{2,1,0:T(8,128)S(1)} %get-tuple-element.85), channel_id=1, source_target_pairs={{0,1},{1,0},{2,3},{3,2},{4,5},{5,4},{6,7},{7,6},{8,9},{9,8},{10,11... | collective-permute-start | bytes 1572872 | tf_op jit(solution)/shard_map/ppermute | solution.py:234
  61.1 6.4 %collective-permute-start.7 = (f32[2,128,256]{2,1,0:T(8,128)S(1)}, f32[2,128,256]{2,1,0:T(8,128)S(1)}, u32[]{:S(2)}, u32[]{:S(2)}) collective-permute-start(f32[2,128,256]{2,1,0:T(8,128)S(1)} %get-tuple-element.76), channel_id=1, source_target_pairs={{0,16},{1,2},{2,1},{3,4},{4,3},{5,6},{6,5},{7,8},{8,7},{9,10},{10,... | collective-permute-start | bytes 786440 | tf_op jit(solution)/shard_map/ppermute | solution.py:231
  62.5 7.7 %collective-permute-start.6 = (f32[2,128,256]{2,1,0:T(8,128)S(1)}, f32[2,128,256]{2,1,0:T(8,128)S(1)}, u32[]{:S(2)}, u32[]{:S(2)}) collective-permute-start(f32[2,128,256]{2,1,0:T(8,128)S(1)} %get-tuple-element.75), channel_id=1, source_target_pairs={{0,16},{1,2},{2,1},{3,4},{4,3},{5,6},{6,5},{7,8},{8,7},{9,10},{10,... | collective-permute-start | bytes 786440 | tf_op jit(solution)/shard_map/ppermute | solution.py:231
  78.1 15.4 %collective-permute-start.14 = (f32[4,128,256]{2,1,0:T(8,128)S(1)}, f32[4,128,256]{2,1,0:T(8,128)S(1)}, u32[]{:S(2)}, u32[]{:S(2)}) collective-permute-start(f32[4,128,256]{2,1,0:T(8,128)S(1)} %get-tuple-element.93), channel_id=1, source_target_pairs={{0,1},{1,0},{2,3},{3,2},{4,5},{5,4},{6,7},{7,6},{8,9},{9,8},{10,11... | collective-permute-start | bytes 1572872 | tf_op jit(solution)/shard_map/ppermute | solution.py:234
  83.3 6.4 %collective-permute-start.10 = (f32[2,128,256]{2,1,0:T(8,128)S(1)}, f32[2,128,256]{2,1,0:T(8,128)S(1)}, u32[]{:S(2)}, u32[]{:S(2)}) collective-permute-start(f32[2,128,256]{2,1,0:T(8,128)S(1)} %get-tuple-element.84), channel_id=1, source_target_pairs={{0,16},{1,2},{2,1},{3,4},{4,3},{5,6},{6,5},{7,8},{8,7},{9,10},{10,... | collective-permute-start | bytes 786440 | tf_op jit(solution)/shard_map/ppermute | solution.py:231
  84.7 7.7 %collective-permute-start.9 = (f32[2,128,256]{2,1,0:T(8,128)S(1)}, f32[2,128,256]{2,1,0:T(8,128)S(1)}, u32[]{:S(2)}, u32[]{:S(2)}) collective-permute-start(f32[2,128,256]{2,1,0:T(8,128)S(1)} %get-tuple-element.83), channel_id=1, source_target_pairs={{0,16},{1,2},{2,1},{3,4},{4,3},{5,6},{6,5},{7,8},{8,7},{9,10},{10,... | collective-permute-start | bytes 786440 | tf_op jit(solution)/shard_map/ppermute | solution.py:231
  100.3 15.4 %collective-permute-start.17 = (f32[4,128,256]{2,1,0:T(8,128)S(1)}, f32[4,128,256]{2,1,0:T(8,128)S(1)}, u32[]{:S(2)}, u32[]{:S(2)}) collective-permute-start(f32[4,128,256]{2,1,0:T(8,128)S(1)} %get-tuple-element.101), channel_id=1, source_target_pairs={{0,1},{1,0},{2,3},{3,2},{4,5},{5,4},{6,7},{7,6},{8,9},{9,8},{10,11... | collective-permute-start | bytes 1572872 | tf_op jit(solution)/shard_map/ppermute | solution.py:234
  105.5 6.4 %collective-permute-start.13 = (f32[2,128,256]{2,1,0:T(8,128)S(1)}, f32[2,128,256]{2,1,0:T(8,128)S(1)}, u32[]{:S(2)}, u32[]{:S(2)}) collective-permute-start(f32[2,128,256]{2,1,0:T(8,128)S(1)} %get-tuple-element.92), channel_id=1, source_target_pairs={{0,16},{1,2},{2,1},{3,4},{4,3},{5,6},{6,5},{7,8},{8,7},{9,10},{10,... | collective-permute-start | bytes 786440 | tf_op jit(solution)/shard_map/ppermute | solution.py:231
  106.9 7.7 %collective-permute-start.12 = (f32[2,128,256]{2,1,0:T(8,128)S(1)}, f32[2,128,256]{2,1,0:T(8,128)S(1)}, u32[]{:S(2)}, u32[]{:S(2)}) collective-permute-start(f32[2,128,256]{2,1,0:T(8,128)S(1)} %get-tuple-element.91), channel_id=1, source_target_pairs={{0,16},{1,2},{2,1},{3,4},{4,3},{5,6},{6,5},{7,8},{8,7},{9,10},{10,... | collective-permute-start | bytes 786440 | tf_op jit(solution)/shard_map/ppermute | solution.py:231
  122.5 15.4 %collective-permute-start.20 = (f32[4,128,256]{2,1,0:T(8,128)S(1)}, f32[4,128,256]{2,1,0:T(8,128)S(1)}, u32[]{:S(2)}, u32[]{:S(2)}) collective-permute-start(f32[4,128,256]{2,1,0:T(8,128)S(1)} %get-tuple-element.109), channel_id=1, source_target_pairs={{0,1},{1,0},{2,3},{3,2},{4,5},{5,4},{6,7},{7,6},{8,9},{9,8},{10,11... | collective-permute-start | bytes 1572872 | tf_op jit(solution)/shard_map/ppermute | solution.py:234
  127.7 6.4 %collective-permute-start.16 = (f32[2,128,256]{2,1,0:T(8,128)S(1)}, f32[2,128,256]{2,1,0:T(8,128)S(1)}, u32[]{:S(2)}, u32[]{:S(2)}) collective-permute-start(f32[2,128,256]{2,1,0:T(8,128)S(1)} %get-tuple-element.100), channel_id=1, source_target_pairs={{0,16},{1,2},{2,1},{3,4},{4,3},{5,6},{6,5},{7,8},{8,7},{9,10},{10,... | collective-permute-start | bytes 786440 | tf_op jit(solution)/shard_map/ppermute | solution.py:231
  129.1 7.7 %collective-permute-start.15 = (f32[2,128,256]{2,1,0:T(8,128)S(1)}, f32[2,128,256]{2,1,0:T(8,128)S(1)}, u32[]{:S(2)}, u32[]{:S(2)}) collective-permute-start(f32[2,128,256]{2,1,0:T(8,128)S(1)} %get-tuple-element.99), channel_id=1, source_target_pairs={{0,16},{1,2},{2,1},{3,4},{4,3},{5,6},{6,5},{7,8},{8,7},{9,10},{10,... | collective-permute-start | bytes 786440 | tf_op jit(solution)/shard_map/ppermute | solution.py:231
  144.9 16.9 %collective-permute-start.23 = (f32[4,128,256]{2,1,0:T(8,128)S(1)}, f32[4,128,256]{2,1,0:T(8,128)S(1)}, u32[]{:S(2)}, u32[]{:S(2)}) collective-permute-start(f32[4,128,256]{2,1,0:T(8,128)S(1)} %get-tuple-element.117), channel_id=1, source_target_pairs={{0,1},{1,0},{2,3},{3,2},{4,5},{5,4},{6,7},{7,6},{8,9},{9,8},{10,11... | collective-permute-start | bytes 1572872 | tf_op jit(solution)/shard_map/ppermute | solution.py:234
  150.0 6.4 %collective-permute-start.19 = (f32[2,128,256]{2,1,0:T(8,128)S(1)}, f32[2,128,256]{2,1,0:T(8,128)S(1)}, u32[]{:S(2)}, u32[]{:S(2)}) collective-permute-start(f32[2,128,256]{2,1,0:T(8,128)S(1)} %get-tuple-element.108), channel_id=1, source_target_pairs={{0,16},{1,2},{2,1},{3,4},{4,3},{5,6},{6,5},{7,8},{8,7},{9,10},{10,... | collective-permute-start | bytes 786440 | tf_op jit(solution)/shard_map/ppermute | solution.py:231
  151.5 7.7 %collective-permute-start.18 = (f32[2,128,256]{2,1,0:T(8,128)S(1)}, f32[2,128,256]{2,1,0:T(8,128)S(1)}, u32[]{:S(2)}, u32[]{:S(2)}) collective-permute-start(f32[2,128,256]{2,1,0:T(8,128)S(1)} %get-tuple-element.107), channel_id=1, source_target_pairs={{0,16},{1,2},{2,1},{3,4},{4,3},{5,6},{6,5},{7,8},{8,7},{9,10},{10,... | collective-permute-start | bytes 786440 | tf_op jit(solution)/shard_map/ppermute | solution.py:231
  157.4 12.0 %collective-permute-start.22 = (f32[2,128,256]{2,1,0:T(8,128)S(1)}, f32[2,128,256]{2,1,0:T(8,128)S(1)}, u32[]{:S(2)}, u32[]{:S(2)}) collective-permute-start(f32[2,128,256]{2,1,0:T(8,128)S(1)} %get-tuple-element.116), channel_id=1, source_target_pairs={{0,16},{1,2},{2,1},{3,4},{4,3},{5,6},{6,5},{7,8},{8,7},{9,10},{10,... | collective-permute-start | bytes 786440 | tf_op jit(solution)/shard_map/ppermute | solution.py:231
  160.2 10.1 %collective-permute-start.21 = (f32[2,128,256]{2,1,0:T(8,128)S(1)}, f32[2,128,256]{2,1,0:T(8,128)S(1)}, u32[]{:S(2)}, u32[]{:S(2)}) collective-permute-start(f32[2,128,256]{2,1,0:T(8,128)S(1)} %get-tuple-element.115), channel_id=1, source_target_pairs={{0,16},{1,2},{2,1},{3,4},{4,3},{5,6},{6,5},{7,8},{8,7},{9,10},{10,... | collective-permute-start | bytes 786440 | tf_op jit(solution)/shard_map/ppermute | solution.py:231
  175.0 12.6 %collective-permute-start.24 = (f32[8,256]{1,0:T(8,128)S(1)}, f32[8,256]{1,0:T(8,128)S(1)}, u32[]{:S(2)}, u32[]{:S(2)}) collective-permute-start(f32[8,256]{1,0:T(8,128)S(1)} %get-tuple-element.125), channel_id=1, source_target_pairs={{0,1},{1,0},{2,3},{3,2},{4,5},{5,4},{6,7},{7,6},{8,9},{9,8},{10,11... | collective-permute-start | bytes 24584 | tf_op jit(solution)/shard_map/ppermute | solution.py:282
  (13 other events, 44.9 us)

commit v2 on v1

v2 whole, which is shorter than its diff:
```python
import functools

import jax
import jax.numpy as jnp
from jax import lax
from jax.experimental import pallas as pl
from jax.experimental.pallas import tpu as pltpu
from jax.sharding import PartitionSpec as P

F32 = jnp.float32
BF16 = jnp.bfloat16
VMEM = pl.BlockSpec(memory_space=pltpu.VMEM)
SMEM = pl.BlockSpec(memory_space=pltpu.SMEM)
ANY = pl.BlockSpec(memory_space=pl.ANY)
EDGE = 2
CHUNKS = 4


def held(*dims):
    return pltpu.VMEM(dims, F32)


def in_hbm(array):
    return pltpu.with_memory_space_constraint(array, pltpu.HBM)


def call(body, outs, ins, aliases=None, scratch=(), flops=0, moved=0, limit=6 << 20, out_spec=VMEM):
    return pl.pallas_call(
        body,
        out_shape=outs,
        in_specs=ins,
        out_specs=jax.tree.map(lambda _: out_spec, outs),
        scratch_shapes=scratch,
        input_output_aliases=aliases or {},
        compiler_params=pltpu.CompilerParams(vmem_limit_bytes=limit),
        cost_estimate=pl.CostEstimate(flops=flops, bytes_accessed=moved, transcendentals=0),
    )


def orientation(planes, far):
    odd = lax.rem(lax.axis_index("gx"), 2)
    sign = 2 * odd - 1
    base = (1 - odd) * (planes - 1)
    return (base + sign * (planes - 1), -sign) if far else (base, sign)


def pack_body(shots, planes, start, *refs):
    outs, sems = refs[:-1], refs[-1]
    started = []
    for far in (True, False):
        base, sign = orientation(planes, far)
        for s in range(shots):
            for d in range(EDGE):
                target = outs[s].at[d] if far else outs[shots].at[s * EDGE + d]
                copy = pltpu.make_async_copy(start.at[s, base + sign * d], target, sems.at[len(started)])
                copy.start()
                started.append(copy)
    for copy in started:
        copy.wait()


def band(rows, columns, center):
    row = lax.broadcasted_iota(jnp.int32, (rows, columns), 0)
    column = lax.broadcasted_iota(jnp.int32, (rows, columns), 1)
    apart = jnp.abs(row - lax.rem(column, rows))
    return jnp.where(apart == 0, center, jnp.where(apart == 1, 16.0, jnp.where(apart == 2, -1.0, 0.0))).astype(BF16)


def tables_body(planes, spots, wavelet, probes, along_z, along_y, weights, force, edge_force, spot_mask, spot_plane):
    along_z[...] = band(*along_z.shape, -60.0)
    along_y[...] = band(*along_y.shape, -30.0)
    steps, shots, frames = weights.shape[:3]
    base, sign = orientation(planes, False)
    tile = weights.shape[3:]
    for s in range(shots):
        own = (spots[s, 0] - lax.axis_index("gx") * planes - base) * sign
        spot_plane[s] = jnp.full(tile, own, jnp.int32).astype(F32)
        rows = lax.broadcasted_iota(jnp.int32, spot_mask.shape[1:], 0)
        columns = lax.broadcasted_iota(jnp.int32, spot_mask.shape[1:], 1)
        spot_mask[s] = jnp.where((rows == spots[s, 1]) & (columns == spots[s, 2]), 1.0, 0.0)
        for t in range(steps):
            force[t, s] = jnp.full(tile, wavelet[s, t], F32)
            for k in range(EDGE):
                edge_force[t, s, k] = jnp.full(tile, jnp.where(own == planes - 1 - k, wavelet[s, t], 0.0), F32)
            for k in range(frames):
                weights[t, s, k] = jnp.full(tile, probes[s, t, k], F32)


def spread(plane, tile):
    rows, columns = plane.shape
    height, width = tile.shape
    parts = [
        (plane[:, at : at + width].reshape(rows // height, height, width) * tile[None]).reshape(rows, width)
        for at in range(0, columns, width)
    ]
    return jnp.concatenate(parts, axis=1)


def dot(a, b):
    return lax.dot_general(a, b, (((1,), (0,)), ((), ())), preferred_element_type=F32)


def advance(down2, down1, mid, up1, up2, last, scaled, along_z, along_y):
    high = mid.astype(BF16)
    low = (mid - high.astype(F32)).astype(BF16)
    total = dot(high, along_z) + dot(low, along_z) + dot(along_y, jnp.concatenate([high, low], axis=0))
    total = total + (16.0 * (down1 + up1) - (down2 + up2))
    return 2.0 * mid - last + scaled * total


def main_body(shots, planes, instant, closing, *refs):
    refs = list(refs)

    def take(count):
        taken = refs[:count]
        del refs[:count]
        return taken

    opening = instant == 0
    along_z, along_y, spot_plane, spot_mask, force, ghost = take(6)
    if opening:
        sources = take(4)
        ahead, send, field, last, courant, sketches = take(6)
        sems = refs[0]
        slab = planes // CHUNKS
        odd = lax.rem(lax.axis_index("gx"), 2)
        copies = []
        for c in range(CHUNKS):
            first = odd * (c * slab) + (1 - odd) * (planes - slab - c * slab)
            span = pl.ds(first, slab)
            copies.append([
                pltpu.make_async_copy(sources[0].at[:, span], field.at[:, span], sems.at[3 * c]),
                pltpu.make_async_copy(sources[1].at[:, span], last.at[:, span], sems.at[3 * c + 1]),
                pltpu.make_async_copy(sources[2].at[span], courant.at[span], sems.at[3 * c + 2]),
            ])
            for copy in copies[-1]:
                copy.start()
        drawing = pltpu.make_async_copy(sources[3], sketches, sems.at[3 * CHUNKS])
        drawing.start()
    else:
        field, last, courant, weights, sketches = take(5)
        before = take(2) if len(refs) > 4 else None
        ahead, send, image, light = take(4)
    base, sign = orientation(planes, False)

    def at(j):
        return base + sign * j

    def now(s, j):
        return ghost[s * EDGE - 1 - j] if isinstance(j, int) and j < 0 else field[s, at(j)]

    def step(j):
        scaled = courant[at(j)] * (1.0 / 12.0)
        for s in range(shots):
            five = [now(s, j + d) for d in (-2, -1, 0, 1, 2)]
            ahead[s, at(j)] = advance(*five, last[s, at(j)], scaled, along_z[...], along_y[...])

    def body(j, carry):
        step(j)
        return carry

    if opening:
        for c in range(CHUNKS):
            for copy in copies[c]:
                copy.wait()
            if c == 0:
                for j in range(EDGE):
                    step(j)
            low, high = (EDGE, slab - EDGE) if c == 0 else (c * slab - EDGE, (c + 1) * slab - EDGE)
            lax.fori_loop(low, high, body, 0, unroll=2)
    else:
        for j in range(EDGE):
            step(j)
        lax.fori_loop(EDGE, planes - EDGE, body, 0, unroll=2)
    for s in range(shots):
        own = jnp.max(spot_plane[s]).astype(jnp.int32)

        @pl.when((own >= 0) & (own < planes - EDGE))
        def _():
            plane = jnp.clip(at(own), 0, planes - 1)
            ahead[s, plane] = ahead[s, plane] + spread(spot_mask[s], force[instant, s])

    if not closing:
        for s in range(shots):
            for d in range(EDGE):
                send[s * EDGE + d] = ahead[s, at(d)]
    if opening:
        drawing.wait()
    else:
        done = [(field, weights.at[instant - 1])]
        if closing:
            odd = lax.rem(lax.axis_index("gx"), 2)
            ready = done + [(ahead, weights.at[instant])]
            add_image((1 - odd) * EDGE, planes - EDGE, ready, sketches, before, image, light)
            add_image(odd * (planes - EDGE), EDGE, done, sketches, before, image, light)
        else:
            add_image(0, planes, done, sketches, before, image, light)


def far_body(instant, shot, planes, along_z, along_y, edge_force, spot_mask, ghost, field, last, courant, partial, ahead, *refs):
    base, sign = orientation(planes, True)
    index = lax.axis_index("gx")
    inner = (index > 0) & (index < lax.axis_size("gx") - 1)

    def at(k):
        return base + sign * k

    def now(k):
        return jnp.where(inner, ghost[-1 - k], 0.0) if k < 0 else field[shot, at(k)]

    for k in range(EDGE):
        five = [now(k + d) for d in (-2, -1, 0, 1, 2)]
        value = advance(*five, last[shot, at(k)], courant[at(k)] * (1.0 / 12.0), along_z[...], along_y[...])
        value = value + spread(spot_mask[shot], edge_force[instant, shot, k])
        ahead[shot, at(k)] = value
        if refs:
            refs[0][k] = value


def add_image(low, count, steps, sketches, before, image_out, light_out):
    shots, frames = sketches.shape[:2]
    breadth, height = image_out.shape[1:]
    rows, columns = 16, 128
    down, across = breadth // rows, height // columns

    def tiles(value):
        return value.reshape(rows // 8, 8, columns)

    def body(number, carry):
        p = low + number // down
        row = pl.ds(pl.multiple_of((number % down) * rows, rows), rows)
        for c in range(across):
            column = pl.ds(c * columns, columns)
            image = light = None
            if before is not None:
                image, light = tiles(before[0][p, row, column]), tiles(before[1][p, row, column])
            for s in range(shots):
                drawn = [tiles(sketches[s, k, p, row, column].astype(F32)) for k in range(frames)]
                for field, weights in steps:
                    value = tiles(field[s, p, row, column])
                    weighted = weights[s, 0][None] * drawn[0]
                    for k in range(1, frames):
                        weighted = weighted + weights[s, k][None] * drawn[k]
                    image = weighted * value if image is None else image + weighted * value
                    light = value * value if light is None else light + value * value
            image_out[p, row, column] = image.reshape(rows, columns)
            light_out[p, row, column] = light.reshape(rows, columns)
        return carry

    lax.fori_loop(0, count * down, body, 0, unroll=2)


def last_body(planes, field, weights, sketches, image_in, light_in, image, light, most):
    odd = lax.rem(lax.axis_index("gx"), 2)
    add_image(odd * (planes - EDGE), EDGE, [(field, weights.at[weights.shape[0] - 1])], sketches,
              (image_in, light_in), image, light)
    breadth, height = light.shape[1:]

    def highest(p):
        return jnp.max(light[p].reshape(breadth // 8, 8, height), axis=0)

    most[...] = lax.fori_loop(1, planes, lambda p, so_far: jnp.maximum(so_far, highest(p)), highest(0))


def divide_body(planes, image, light, most, out, quotient, sems):
    largest = 0.1 * jnp.max(most[...])
    slab = planes // CHUNKS
    copies = []
    for c in range(CHUNKS):
        def body(p, carry):
            quotient[p] = image[p] / (light[p] + largest)
            return carry

        lax.fori_loop(c * slab, (c + 1) * slab, body, 0)
        span = pl.ds(c * slab, slab)
        copies.append(pltpu.make_async_copy(quotient.at[span], out.at[span], sems.at[c]))
        copies[-1].start()
    for copy in copies:
        copy.wait()


def per_device(courant, sketches, probes, source_spot, wavelet, adjoint_before, adjoint_start):
    shots, planes, breadth, height = adjoint_start.shape
    frames, steps = sketches.shape[1], wavelet.shape[1]
    count, areas = lax.axis_size("gx"), lax.axis_size("survey")

    near_pairs = [(i, i ^ 1) for i in range(count)]
    far_pairs = []
    for area in range(areas):
        for i in range(count):
            other = i + 1 if i % 2 else i - 1
            if 0 <= other < count:
                far_pairs.append((area * count + i, area * count + other))
            elif areas % 2 == 0:
                far_pairs.append((area * count + i, (area ^ 1) * count + i))
    plane_bytes = 4 * breadth * height
    whole = held(shots, planes, breadth, height)
    still = held(planes, breadth, height)
    edge = held(EDGE, breadth, height)
    both = held(shots * EDGE, breadth, height)

    def to_far(planes_out):
        return lax.ppermute(planes_out, ("survey", "gx"), far_pairs)

    def to_near(planes_out):
        return lax.ppermute(planes_out, "gx", near_pairs)

    *far, near = call(
        functools.partial(pack_body, shots, planes), (edge,) * shots + (both,), [ANY],
        scratch=[pltpu.SemaphoreType.DMA((2 * shots * EDGE,))], moved=8 * shots * plane_bytes,
    )(in_hbm(adjoint_start))
    far = [to_far(part) for part in far]
    near = to_near(near)
    along_z, along_y, weights, force, edge_force, spot_mask, spot_plane = call(
        functools.partial(tables_body, planes),
        (
            pltpu.VMEM((height, height), BF16), pltpu.VMEM((breadth, 2 * breadth), BF16),
            held(steps, shots, frames, 8, 128), held(steps, shots, 8, 128), held(steps, shots, EDGE, 8, 128),
            held(shots, breadth, height), held(shots, 8, 128),
        ),
        [SMEM] * 3, moved=1 << 20,
    )(source_spot, wavelet, probes)
    images = []
    for instant in range(steps):
        opening, closing = instant == 0, instant == steps - 1
        tables = [along_z, along_y, spot_plane, spot_mask, force, near]
        if opening:
            ahead, near_sent, field, last, courant, sketches = call(
                functools.partial(main_body, shots, planes, 0, False),
                (whole, both, whole, whole, still, pltpu.VMEM(sketches.shape, BF16)), [VMEM] * 6 + [ANY] * 4,
                scratch=[pltpu.SemaphoreType.DMA((3 * CHUNKS + 1,))],
                flops=2 * planes * shots * breadth * height * 512, moved=8 * planes * shots * plane_bytes,
            )(*tables, *(in_hbm(each) for each in (adjoint_start, adjoint_before, courant, sketches)))
        else:
            inputs = [*tables, field, last, courant, weights, sketches, *images]
            ahead, near_sent, *images = call(
                functools.partial(main_body, shots, planes, instant, closing),
                (whole, both, still, still), [VMEM] * len(inputs),
                aliases={len(inputs) - 2: 2, len(inputs) - 1: 3} if images else {},
                flops=2 * planes * shots * breadth * height * 512, moved=8 * planes * shots * plane_bytes,
            )(*inputs)
        if not closing:
            near = to_near(near_sent)
        for shot in range(shots):
            inputs = [along_z, along_y, edge_force, spot_mask, far[shot], field, last, courant, ahead]
            ahead, *sent = call(
                functools.partial(far_body, instant, shot, planes),
                (whole,) if closing else (whole, edge), [VMEM] * len(inputs), aliases={len(inputs) - 1: 0},
                flops=4 * breadth * height * 512, moved=16 * plane_bytes,
            )(*inputs)
            if not closing:
                far[shot] = to_far(sent[0])
        field, last = ahead, field
    image, light, most = call(
        functools.partial(last_body, planes),
        (still, still, held(8, height)), [VMEM] * 5, aliases={3: 0, 4: 1},
        moved=8 * planes * shots * plane_bytes,
    )(field, weights, sketches, *images)
    reach = 1
    while reach < count:
        most = jnp.maximum(most, lax.ppermute(most, "gx", [(i, i ^ reach) for i in range(count)]))
        reach *= 2
    result = call(
        functools.partial(divide_body, planes), pltpu.HBM((planes, breadth, height), F32), [VMEM] * 3,
        scratch=[pltpu.VMEM((planes, breadth, height), F32), pltpu.SemaphoreType.DMA((CHUNKS,))], out_spec=ANY,
        moved=3 * planes * plane_bytes,
    )(image, light, most)
    return result, field


def solution(mesh):
    placed = (
        P("gx", "survey", None),
        P("survey", None, "gx", None, None),
        P("survey", None, None),
        P("survey", None),
        P("survey", None),
        P("survey", "gx", None, None),
        P("survey", "gx", None, None),
    )
    return jax.shard_map(
        per_device,
        mesh=mesh,
        in_specs=placed,
        out_specs=(P("gx", "survey", None), P("survey", "gx", None, None)),
        check_vma=False,
    )
```

time: 202 us -> 187 us (0.926)
  Pallas kernels: 76.6 us -> 64.3 us
  local copies, waits for them, and re-layouts: 8.94 us -> 2.11 us
  waiting for transfers between devices: 49 us -> 53.2 us
    pallas_call x28, Pallas kernels: 76.6 us -> 64.3 us  [the longest x7 48.5 us: per_device(): call(functools.partial(main_body, shots, planes, instant, closing), (whol...]
    unnamed x20 -> x8, local copies, waits for them, and re-layouts: 8.94 us -> 2.11 us
    ppermute x16, waiting for transfers between devices: 41.4 us -> 46.3 us  [to_far(): return lax.ppermute(planes_out, ('survey', 'gx'), far_pairs)]
  transfers between devices with their start and end apart: 28 -> 28, of which waited for: 18 -> 18; matrix products, arithmetic and copies ran while one was open for 1% -> 1% of each run, Pallas kernels for 12% -> 7%
where the time goes in v2:
time: 187 us
  starting transfers between devices  66 us (35%)
  Pallas kernels  64.3 us (34%)
  waiting for transfers between devices  53.2 us (28%)
  local copies, waits for them, and re-layouts  2.11 us (1%)
    pallas_call x7, Pallas kernels, per_device(): call(functools.partial(main_body, shots, planes, instant, closing), (whol...  48.5 us
    ppermute x16, waiting for transfers between devices, to_far(): return lax.ppermute(planes_out, ('survey', 'gx'), far_pairs)  46.3 us
    ppermute x8, starting transfers between devices, to_near(): return lax.ppermute(planes_out, 'gx', near_pairs)  31.8 us
    ppermute x16, starting transfers between devices, to_far(): return lax.ppermute(planes_out, ('survey', 'gx'), far_pairs)  18 us
    ppermute x4, starting transfers between devices, per_device(): lax.ppermute(most, 'gx', [(i, i ^ reach) for i in range(count)])  16.3 us
    pallas_call x1, Pallas kernels, per_device(): call(functools.partial(main_body, shots, planes, 0, False), (whole, both,...  6.59 us
    ppermute x4, waiting for transfers between devices, per_device(): lax.ppermute(most, 'gx', [(i, i ^ reach) for i in range(count)])  6.28 us
    pallas_call x16, Pallas kernels, per_device(): call(functools.partial(far_body, instant, shot, planes), (whole,) if clos...  4.84 us
  transfers between devices with their start and end apart: 28, of which 18 were waited for; matrix products, arithmetic and copies ran while one was open for 1% of the time, Pallas kernels for 7%

profile of v2, /device:TPU:0, one launch (start us, length us, event | category | flops | bytes accessed | tf_op | source)
XLA Modules:
  0.0 186.7 jit_solution(9871031919363568427)
XLA Ops:
  4.1 6.6 %shard_map.88 = (f32[2,16,128,256]{3,2,1,0:T(8,128)S(1)}, f32[4,128,256]{2,1,0:T(8,128)S(1)}, f32[2,16,128,256]{3,2,1,0:T(8,128)S(1)}, f32[2,16,128,256]{3,2,1,0...) custom-call(bf16[256,256]{1,0:T(8,128)(2,1)S(1)} %get-tuple-element.76.refs_0_.along_z, ...), custom_call_target="tpu_custom_call" | custom-call | flops 1073741824 | bytes 33554432 | tf_op jit(solution)/shard_map/pallas_call | solution.py:328
  13.8 4.3 %collective-permute-done.2.ghost = f32[2,128,256]{2,1,0:T(8,128)S(1)} collective-permute-done((f32[2,128,256]{2,1,0:T(8,128)S(1)}, f32[2,128,256]{2,1,0:T(8,128)S(1)}, u32[]{:S(2)}, u32[]{:S(2)}) %collective-permute-start.2) | collective-permute-done | bytes 262176 | tf_op jit(solution)/shard_map/ppermute | solution.py:303
  21.3 6.6 %shard_map.91 = (f32[2,16,128,256]{3,2,1,0:T(8,128)S(1)}, f32[4,128,256]{2,1,0:T(8,128)S(1)}, f32[16,128,256]{2,1,0:T(8,128)S(1)}, f32[16,128,256]{2,1,0:T(8,128)S(1)}) custom-call(bf16[256,256]{1,0:T(8,128)(2,1)S(1)} %get-tuple-element.76.refs_0_.along_z, bf16[128,256]{1,0:T(8,128)(2,1)S(1)} %get-tuple-element.77.refs_1_.along_y, ...), custom_call_target="tpu_custom_call" | custom-call | flops 1073741824 | bytes 33554432 | tf_op jit(solution)/shard_map/pallas_call | solution.py:336
  27.9 4.8 %collective-permute-start.8 = (f32[4,128,256]{2,1,0:T(8,128)S(1)}, f32[4,128,256]{2,1,0:T(8,128)S(1)}, u32[]{:S(2)}, u32[]{:S(2)}) collective-permute-start(f32[4,128,256]{2,1,0:T(8,128)S(1)} %get-tuple-element.101), channel_id=1, source_target_pairs={{0,1},{1,0},{2,3},{3,2},{4,5},{5,4},{6,7},{7,6},{8,9},{9,8},{10,11... | collective-permute-start | bytes 1572872 | tf_op jit(solution)/shard_map/ppermute | solution.py:306
  34.7 4.3 %collective-permute-done.4.ghost = f32[2,128,256]{2,1,0:T(8,128)S(1)} collective-permute-done((f32[2,128,256]{2,1,0:T(8,128)S(1)}, f32[2,128,256]{2,1,0:T(8,128)S(1)}, u32[]{:S(2)}, u32[]{:S(2)}) %collective-permute-start.4) | collective-permute-done | bytes 262176 | tf_op jit(solution)/shard_map/ppermute | solution.py:303
  42.2 6.6 %shard_map.94 = (f32[2,16,128,256]{3,2,1,0:T(8,128)S(1)}, f32[4,128,256]{2,1,0:T(8,128)S(1)}, f32[16,128,256]{2,1,0:T(8,128)S(1)}, f32[16,128,256]{2,1,0:T(8,128)S(1)}) custom-call(bf16[256,256]{1,0:T(8,128)(2,1)S(1)} %get-tuple-element.76.refs_0_.along_z, ...), custom_call_target="tpu_custom_call", output_to_operand_aliasing={{2}: (11, {}), {3}: (12, {})} | custom-call | flops 1073741824 | bytes 33554432 | tf_op jit(solution)/shard_map/pallas_call | solution.py:336
  48.8 5.2 %collective-permute-start.11 = (f32[4,128,256]{2,1,0:T(8,128)S(1)}, f32[4,128,256]{2,1,0:T(8,128)S(1)}, u32[]{:S(2)}, u32[]{:S(2)}) collective-permute-start(f32[4,128,256]{2,1,0:T(8,128)S(1)} %get-tuple-element.109), channel_id=1, source_target_pairs={{0,1},{1,0},{2,3},{3,2},{4,5},{5,4},{6,7},{7,6},{8,9},{9,8},{10,11... | collective-permute-start | bytes 1572872 | tf_op jit(solution)/shard_map/ppermute | solution.py:306
  56.0 4.3 %collective-permute-done.7.ghost = f32[2,128,256]{2,1,0:T(8,128)S(1)} collective-permute-done((f32[2,128,256]{2,1,0:T(8,128)S(1)}, f32[2,128,256]{2,1,0:T(8,128)S(1)}, u32[]{:S(2)}, u32[]{:S(2)}) %collective-permute-start.7) | collective-permute-done | bytes 262176 | tf_op jit(solution)/shard_map/ppermute | solution.py:303
  63.5 6.6 %shard_map.97 = (f32[2,16,128,256]{3,2,1,0:T(8,128)S(1)}, f32[4,128,256]{2,1,0:T(8,128)S(1)}, f32[16,128,256]{2,1,0:T(8,128)S(1)}, f32[16,128,256]{2,1,0:T(8,128)S(1)}) custom-call(bf16[256,256]{1,0:T(8,128)(2,1)S(1)} %get-tuple-element.76.refs_0_.along_z, ...), custom_call_target="tpu_custom_call", output_to_operand_aliasing={{2}: (11, {}), {3}: (12, {})} | custom-call | flops 1073741824 | bytes 33554432 | tf_op jit(solution)/shard_map/pallas_call | solution.py:336
  70.2 5.2 %collective-permute-start.14 = (f32[4,128,256]{2,1,0:T(8,128)S(1)}, f32[4,128,256]{2,1,0:T(8,128)S(1)}, u32[]{:S(2)}, u32[]{:S(2)}) collective-permute-start(f32[4,128,256]{2,1,0:T(8,128)S(1)} %get-tuple-element.117), channel_id=1, source_target_pairs={{0,1},{1,0},{2,3},{3,2},{4,5},{5,4},{6,7},{7,6},{8,9},{9,8},{10,11... | collective-permute-start | bytes 1572872 | tf_op jit(solution)/shard_map/ppermute | solution.py:306
  77.4 4.3 %collective-permute-done.10.ghost = f32[2,128,256]{2,1,0:T(8,128)S(1)} collective-permute-done((f32[2,128,256]{2,1,0:T(8,128)S(1)}, f32[2,128,256]{2,1,0:T(8,128)S(1)}, u32[]{:S(2)}, u32[]{:S(2)}) %collective-permute-start.10) | collective-permute-done | bytes 262176 | tf_op jit(solution)/shard_map/ppermute | solution.py:303
  84.9 6.6 %shard_map.100 = (f32[2,16,128,256]{3,2,1,0:T(8,128)S(1)}, f32[4,128,256]{2,1,0:T(8,128)S(1)}, f32[16,128,256]{2,1,0:T(8,128)S(1)}, f32[16,128,256]{2,1,0:T(8,128)S(1)}) custom-call(bf16[256,256]{1,0:T(8,128)(2,1)S(1)} %get-tuple-element.76.refs_0_.along_z, ...), custom_call_target="tpu_custom_call", output_to_operand_aliasing={{2}: (11, {}), {3}: (12, {})} | custom-call | flops 1073741824 | bytes 33554432 | tf_op jit(solution)/shard_map/pallas_call | solution.py:336
  91.5 5.2 %collective-permute-start.17 = (f32[4,128,256]{2,1,0:T(8,128)S(1)}, f32[4,128,256]{2,1,0:T(8,128)S(1)}, u32[]{:S(2)}, u32[]{:S(2)}) collective-permute-start(f32[4,128,256]{2,1,0:T(8,128)S(1)} %get-tuple-element.125), channel_id=1, source_target_pairs={{0,1},{1,0},{2,3},{3,2},{4,5},{5,4},{6,7},{7,6},{8,9},{9,8},{10,11... | collective-permute-start | bytes 1572872 | tf_op jit(solution)/shard_map/ppermute | solution.py:306
  98.8 4.3 %collective-permute-done.13.ghost = f32[2,128,256]{2,1,0:T(8,128)S(1)} collective-permute-done((f32[2,128,256]{2,1,0:T(8,128)S(1)}, f32[2,128,256]{2,1,0:T(8,128)S(1)}, u32[]{:S(2)}, u32[]{:S(2)}) %collective-permute-start.13) | collective-permute-done | bytes 262176 | tf_op jit(solution)/shard_map/ppermute | solution.py:303
  106.2 6.8 %shard_map.103 = (f32[2,16,128,256]{3,2,1,0:T(8,128)S(1)}, f32[4,128,256]{2,1,0:T(8,128)S(1)}, f32[16,128,256]{2,1,0:T(8,128)S(1)}, f32[16,128,256]{2,1,0:T(8,128)S(1)}) custom-call(bf16[256,256]{1,0:T(8,128)(2,1)S(1)} %get-tuple-element.76.refs_0_.along_z, ...), custom_call_target="tpu_custom_call", output_to_operand_aliasing={{2}: (11, {}), {3}: (12, {})} | custom-call | flops 1073741824 | bytes 33554432 | tf_op jit(solution)/shard_map/pallas_call | solution.py:336
  113.1 5.2 %collective-permute-start.20 = (f32[4,128,256]{2,1,0:T(8,128)S(1)}, f32[4,128,256]{2,1,0:T(8,128)S(1)}, u32[]{:S(2)}, u32[]{:S(2)}) collective-permute-start(f32[4,128,256]{2,1,0:T(8,128)S(1)} %get-tuple-element.133), channel_id=1, source_target_pairs={{0,1},{1,0},{2,3},{3,2},{4,5},{5,4},{6,7},{7,6},{8,9},{9,8},{10,11... | collective-permute-start | bytes 1572872 | tf_op jit(solution)/shard_map/ppermute | solution.py:306
  120.3 4.3 %collective-permute-done.16.ghost = f32[2,128,256]{2,1,0:T(8,128)S(1)} collective-permute-done((f32[2,128,256]{2,1,0:T(8,128)S(1)}, f32[2,128,256]{2,1,0:T(8,128)S(1)}, u32[]{:S(2)}, u32[]{:S(2)}) %collective-permute-start.16) | collective-permute-done | bytes 262176 | tf_op jit(solution)/shard_map/ppermute | solution.py:303
  127.8 6.6 %shard_map.106 = (f32[2,16,128,256]{3,2,1,0:T(8,128)S(1)}, f32[4,128,256]{2,1,0:T(8,128)S(1)}, f32[16,128,256]{2,1,0:T(8,128)S(1)}, f32[16,128,256]{2,1,0:T(8,128)S(1)}) custom-call(bf16[256,256]{1,0:T(8,128)(2,1)S(1)} %get-tuple-element.76.refs_0_.along_z, ...), custom_call_target="tpu_custom_call", output_to_operand_aliasing={{2}: (11, {}), {3}: (12, {})} | custom-call | flops 1073741824 | bytes 33554432 | tf_op jit(solution)/shard_map/pallas_call | solution.py:336
  134.4 5.2 %collective-permute-start.23 = (f32[4,128,256]{2,1,0:T(8,128)S(1)}, f32[4,128,256]{2,1,0:T(8,128)S(1)}, u32[]{:S(2)}, u32[]{:S(2)}) collective-permute-start(f32[4,128,256]{2,1,0:T(8,128)S(1)} %get-tuple-element.141), channel_id=1, source_target_pairs={{0,1},{1,0},{2,3},{3,2},{4,5},{5,4},{6,7},{7,6},{8,9},{9,8},{10,11... | collective-permute-start | bytes 1572872 | tf_op jit(solution)/shard_map/ppermute | solution.py:306
  141.7 4.3 %collective-permute-done.19.ghost = f32[2,128,256]{2,1,0:T(8,128)S(1)} collective-permute-done((f32[2,128,256]{2,1,0:T(8,128)S(1)}, f32[2,128,256]{2,1,0:T(8,128)S(1)}, u32[]{:S(2)}, u32[]{:S(2)}) %collective-permute-start.19) | collective-permute-done | bytes 262176 | tf_op jit(solution)/shard_map/ppermute | solution.py:303
  150.7 8.5 %shard_map.109 = (f32[2,16,128,256]{3,2,1,0:T(8,128)S(1)}, f32[4,128,256]{2,1,0:T(8,128)}, f32[16,128,256]{2,1,0:T(8,128)S(1)}, f32[16,128,256]{2,1,0:T(8,128)S(1)}) custom-call(bf16[256,256]{1,0:T(8,128)(2,1)S(1)} %get-tuple-element.76.refs_0_.along_z, ...), custom_call_target="tpu_custom_call", output_to_operand_aliasing={{2}: (11, {}), {3}: (12, {})} | custom-call | flops 1073741824 | bytes 33554432 | tf_op jit(solution)/shard_map/pallas_call | solution.py:336
  160.4 11.8 %collective-permute-start.24 = (f32[8,256]{1,0:T(8,128)S(1)}, f32[8,256]{1,0:T(8,128)S(1)}, u32[]{:S(2)}, u32[]{:S(2)}) collective-permute-start(f32[8,256]{1,0:T(8,128)S(1)} %get-tuple-element.149), channel_id=1, source_target_pairs={{0,1},{1,0},{2,3},{3,2},{4,5},{5,4},{6,7},{7,6},{8,9},{9,8},{10,11... | collective-permute-start | bytes 24584 | tf_op jit(solution)/shard_map/ppermute | solution.py:361
  173.3 3.4 %collective-permute-done.25 = f32[8,256]{1,0:T(8,128)S(1)} collective-permute-done((f32[8,256]{1,0:T(8,128)S(1)}, f32[8,256]{1,0:T(8,128)S(1)}, u32[]{:S(2)}, u32[]{:S(2)}) %collective-permute-start.25) | collective-permute-done | bytes 8224 | tf_op jit(solution)/shard_map/ppermute | solution.py:361
  180.3 2.6 %collective-permute-start.27 = (f32[8,256]{1,0:T(8,128)S(1)}, f32[8,256]{1,0:T(8,128)S(1)}, u32[]{:S(2)}, u32[]{:S(2)}) collective-permute-start(f32[8,256]{1,0:T(8,128)S(1)} %max.14), channel_id=1, source_target_pairs={{0,8},{1,9},{2,10},{3,11},{4,12},{5,13},{6,14},{7,15},{8,0},{9,1},... | collective-permute-start | bytes 24584 | tf_op jit(solution)/shard_map/ppermute | solution.py:361
  (72 shorter events, 51.5 us)
Async XLA Ops:
  10.7 10.5 %collective-permute-start.5 = (f32[4,128,256]{2,1,0:T(8,128)S(1)}, f32[4,128,256]{2,1,0:T(8,128)S(1)}, u32[]{:S(2)}, u32[]{:S(2)}) collective-permute-start(f32[4,128,256]{2,1,0:T(8,128)S(1)} %get-tuple-element.93), channel_id=1, source_target_pairs={{0,1},{1,0},{2,3},{3,2},{4,5},{5,4},{6,7},{7,6},{8,9},{9,8},{10,11... | collective-permute-start | bytes 1572872 | tf_op jit(solution)/shard_map/ppermute | solution.py:306
  11.2 7.0 %collective-permute-start.2 = (f32[2,128,256]{2,1,0:T(8,128)S(1)}, f32[2,128,256]{2,1,0:T(8,128)S(1)}, u32[]{:S(2)}, u32[]{:S(2)}) collective-permute-start(f32[2,128,256]{2,1,0:T(8,128)S(1)} %get-tuple-element.87), channel_id=1, source_target_pairs={{0,16},{1,2},{2,1},{3,4},{4,3},{5,6},{6,5},{7,8},{8,7},{9,10},{10,... | collective-permute-start | bytes 786440 | tf_op jit(solution)/shard_map/ppermute | solution.py:303
  13.8 7.2 %collective-permute-start = (f32[2,128,256]{2,1,0:T(8,128)S(1)}, f32[2,128,256]{2,1,0:T(8,128)S(1)}, u32[]{:S(2)}, u32[]{:S(2)}) collective-permute-start(f32[2,128,256]{2,1,0:T(8,128)S(1)} %get-tuple-element.80), channel_id=1, source_target_pairs={{0,16},{1,2},{2,1},{3,4},{4,3},{5,6},{6,5},{7,8},{8,7},{9,10},{10,... | collective-permute-start | bytes 786440 | tf_op jit(solution)/shard_map/ppermute | solution.py:303
  27.9 14.3 %collective-permute-start.8 = (f32[4,128,256]{2,1,0:T(8,128)S(1)}, f32[4,128,256]{2,1,0:T(8,128)S(1)}, u32[]{:S(2)}, u32[]{:S(2)}) collective-permute-start(f32[4,128,256]{2,1,0:T(8,128)S(1)} %get-tuple-element.101), channel_id=1, source_target_pairs={{0,1},{1,0},{2,3},{3,2},{4,5},{5,4},{6,7},{7,6},{8,9},{9,8},{10,11... | collective-permute-start | bytes 1572872 | tf_op jit(solution)/shard_map/ppermute | solution.py:306
  32.7 6.4 %collective-permute-start.4 = (f32[2,128,256]{2,1,0:T(8,128)S(1)}, f32[2,128,256]{2,1,0:T(8,128)S(1)}, u32[]{:S(2)}, u32[]{:S(2)}) collective-permute-start(f32[2,128,256]{2,1,0:T(8,128)S(1)} %get-tuple-element.92), channel_id=1, source_target_pairs={{0,16},{1,2},{2,1},{3,4},{4,3},{5,6},{6,5},{7,8},{8,7},{9,10},{10,... | collective-permute-start | bytes 786440 | tf_op jit(solution)/shard_map/ppermute | solution.py:303
  34.2 7.7 %collective-permute-start.3 = (f32[2,128,256]{2,1,0:T(8,128)S(1)}, f32[2,128,256]{2,1,0:T(8,128)S(1)}, u32[]{:S(2)}, u32[]{:S(2)}) collective-permute-start(f32[2,128,256]{2,1,0:T(8,128)S(1)} %get-tuple-element.90), channel_id=1, source_target_pairs={{0,16},{1,2},{2,1},{3,4},{4,3},{5,6},{6,5},{7,8},{8,7},{9,10},{10,... | collective-permute-start | bytes 786440 | tf_op jit(solution)/shard_map/ppermute | solution.py:303
  48.8 14.7 %collective-permute-start.11 = (f32[4,128,256]{2,1,0:T(8,128)S(1)}, f32[4,128,256]{2,1,0:T(8,128)S(1)}, u32[]{:S(2)}, u32[]{:S(2)}) collective-permute-start(f32[4,128,256]{2,1,0:T(8,128)S(1)} %get-tuple-element.109), channel_id=1, source_target_pairs={{0,1},{1,0},{2,3},{3,2},{4,5},{5,4},{6,7},{7,6},{8,9},{9,8},{10,11... | collective-permute-start | bytes 1572872 | tf_op jit(solution)/shard_map/ppermute | solution.py:306
  54.0 6.4 %collective-permute-start.7 = (f32[2,128,256]{2,1,0:T(8,128)S(1)}, f32[2,128,256]{2,1,0:T(8,128)S(1)}, u32[]{:S(2)}, u32[]{:S(2)}) collective-permute-start(f32[2,128,256]{2,1,0:T(8,128)S(1)} %get-tuple-element.100), channel_id=1, source_target_pairs={{0,16},{1,2},{2,1},{3,4},{4,3},{5,6},{6,5},{7,8},{8,7},{9,10},{10,... | collective-permute-start | bytes 786440 | tf_op jit(solution)/shard_map/ppermute | solution.py:303
  55.5 7.7 %collective-permute-start.6 = (f32[2,128,256]{2,1,0:T(8,128)S(1)}, f32[2,128,256]{2,1,0:T(8,128)S(1)}, u32[]{:S(2)}, u32[]{:S(2)}) collective-permute-start(f32[2,128,256]{2,1,0:T(8,128)S(1)} %get-tuple-element.98), channel_id=1, source_target_pairs={{0,16},{1,2},{2,1},{3,4},{4,3},{5,6},{6,5},{7,8},{8,7},{9,10},{10,... | collective-permute-start | bytes 786440 | tf_op jit(solution)/shard_map/ppermute | solution.py:303
  70.2 14.7 %collective-permute-start.14 = (f32[4,128,256]{2,1,0:T(8,128)S(1)}, f32[4,128,256]{2,1,0:T(8,128)S(1)}, u32[]{:S(2)}, u32[]{:S(2)}) collective-permute-start(f32[4,128,256]{2,1,0:T(8,128)S(1)} %get-tuple-element.117), channel_id=1, source_target_pairs={{0,1},{1,0},{2,3},{3,2},{4,5},{5,4},{6,7},{7,6},{8,9},{9,8},{10,11... | collective-permute-start | bytes 1572872 | tf_op jit(solution)/shard_map/ppermute | solution.py:306
  75.4 6.4 %collective-permute-start.10 = (f32[2,128,256]{2,1,0:T(8,128)S(1)}, f32[2,128,256]{2,1,0:T(8,128)S(1)}, u32[]{:S(2)}, u32[]{:S(2)}) collective-permute-start(f32[2,128,256]{2,1,0:T(8,128)S(1)} %get-tuple-element.108), channel_id=1, source_target_pairs={{0,16},{1,2},{2,1},{3,4},{4,3},{5,6},{6,5},{7,8},{8,7},{9,10},{10,... | collective-permute-start | bytes 786440 | tf_op jit(solution)/shard_map/ppermute | solution.py:303
  76.9 7.7 %collective-permute-start.9 = (f32[2,128,256]{2,1,0:T(8,128)S(1)}, f32[2,128,256]{2,1,0:T(8,128)S(1)}, u32[]{:S(2)}, u32[]{:S(2)}) collective-permute-start(f32[2,128,256]{2,1,0:T(8,128)S(1)} %get-tuple-element.106), channel_id=1, source_target_pairs={{0,16},{1,2},{2,1},{3,4},{4,3},{5,6},{6,5},{7,8},{8,7},{9,10},{10,... | collective-permute-start | bytes 786440 | tf_op jit(solution)/shard_map/ppermute | solution.py:303
  91.5 14.7 %collective-permute-start.17 = (f32[4,128,256]{2,1,0:T(8,128)S(1)}, f32[4,128,256]{2,1,0:T(8,128)S(1)}, u32[]{:S(2)}, u32[]{:S(2)}) collective-permute-start(f32[4,128,256]{2,1,0:T(8,128)S(1)} %get-tuple-element.125), channel_id=1, source_target_pairs={{0,1},{1,0},{2,3},{3,2},{4,5},{5,4},{6,7},{7,6},{8,9},{9,8},{10,11... | collective-permute-start | bytes 1572872 | tf_op jit(solution)/shard_map/ppermute | solution.py:306
  96.7 6.4 %collective-permute-start.13 = (f32[2,128,256]{2,1,0:T(8,128)S(1)}, f32[2,128,256]{2,1,0:T(8,128)S(1)}, u32[]{:S(2)}, u32[]{:S(2)}) collective-permute-start(f32[2,128,256]{2,1,0:T(8,128)S(1)} %get-tuple-element.116), channel_id=1, source_target_pairs={{0,16},{1,2},{2,1},{3,4},{4,3},{5,6},{6,5},{7,8},{8,7},{9,10},{10,... | collective-permute-start | bytes 786440 | tf_op jit(solution)/shard_map/ppermute | solution.py:303
  98.2 7.7 %collective-permute-start.12 = (f32[2,128,256]{2,1,0:T(8,128)S(1)}, f32[2,128,256]{2,1,0:T(8,128)S(1)}, u32[]{:S(2)}, u32[]{:S(2)}) collective-permute-start(f32[2,128,256]{2,1,0:T(8,128)S(1)} %get-tuple-element.114), channel_id=1, source_target_pairs={{0,16},{1,2},{2,1},{3,4},{4,3},{5,6},{6,5},{7,8},{8,7},{9,10},{10,... | collective-permute-start | bytes 786440 | tf_op jit(solution)/shard_map/ppermute | solution.py:303
  113.1 14.7 %collective-permute-start.20 = (f32[4,128,256]{2,1,0:T(8,128)S(1)}, f32[4,128,256]{2,1,0:T(8,128)S(1)}, u32[]{:S(2)}, u32[]{:S(2)}) collective-permute-start(f32[4,128,256]{2,1,0:T(8,128)S(1)} %get-tuple-element.133), channel_id=1, source_target_pairs={{0,1},{1,0},{2,3},{3,2},{4,5},{5,4},{6,7},{7,6},{8,9},{9,8},{10,11... | collective-permute-start | bytes 1572872 | tf_op jit(solution)/shard_map/ppermute | solution.py:306
  118.3 6.4 %collective-permute-start.16 = (f32[2,128,256]{2,1,0:T(8,128)S(1)}, f32[2,128,256]{2,1,0:T(8,128)S(1)}, u32[]{:S(2)}, u32[]{:S(2)}) collective-permute-start(f32[2,128,256]{2,1,0:T(8,128)S(1)} %get-tuple-element.124), channel_id=1, source_target_pairs={{0,16},{1,2},{2,1},{3,4},{4,3},{5,6},{6,5},{7,8},{8,7},{9,10},{10,... | collective-permute-start | bytes 786440 | tf_op jit(solution)/shard_map/ppermute | solution.py:303
  119.8 7.7 %collective-permute-start.15 = (f32[2,128,256]{2,1,0:T(8,128)S(1)}, f32[2,128,256]{2,1,0:T(8,128)S(1)}, u32[]{:S(2)}, u32[]{:S(2)}) collective-permute-start(f32[2,128,256]{2,1,0:T(8,128)S(1)} %get-tuple-element.122), channel_id=1, source_target_pairs={{0,16},{1,2},{2,1},{3,4},{4,3},{5,6},{6,5},{7,8},{8,7},{9,10},{10,... | collective-permute-start | bytes 786440 | tf_op jit(solution)/shard_map/ppermute | solution.py:303
  134.4 16.3 %collective-permute-start.23 = (f32[4,128,256]{2,1,0:T(8,128)S(1)}, f32[4,128,256]{2,1,0:T(8,128)S(1)}, u32[]{:S(2)}, u32[]{:S(2)}) collective-permute-start(f32[4,128,256]{2,1,0:T(8,128)S(1)} %get-tuple-element.141), channel_id=1, source_target_pairs={{0,1},{1,0},{2,3},{3,2},{4,5},{5,4},{6,7},{7,6},{8,9},{9,8},{10,11... | collective-permute-start | bytes 1572872 | tf_op jit(solution)/shard_map/ppermute | solution.py:306
  139.6 6.4 %collective-permute-start.19 = (f32[2,128,256]{2,1,0:T(8,128)S(1)}, f32[2,128,256]{2,1,0:T(8,128)S(1)}, u32[]{:S(2)}, u32[]{:S(2)}) collective-permute-start(f32[2,128,256]{2,1,0:T(8,128)S(1)} %get-tuple-element.132), channel_id=1, source_target_pairs={{0,16},{1,2},{2,1},{3,4},{4,3},{5,6},{6,5},{7,8},{8,7},{9,10},{10,... | collective-permute-start | bytes 786440 | tf_op jit(solution)/shard_map/ppermute | solution.py:303
  141.2 7.7 %collective-permute-start.18 = (f32[2,128,256]{2,1,0:T(8,128)S(1)}, f32[2,128,256]{2,1,0:T(8,128)S(1)}, u32[]{:S(2)}, u32[]{:S(2)}) collective-permute-start(f32[2,128,256]{2,1,0:T(8,128)S(1)} %get-tuple-element.130), channel_id=1, source_target_pairs={{0,16},{1,2},{2,1},{3,4},{4,3},{5,6},{6,5},{7,8},{8,7},{9,10},{10,... | collective-permute-start | bytes 786440 | tf_op jit(solution)/shard_map/ppermute | solution.py:303
  146.3 12.9 %collective-permute-start.22 = (f32[2,128,256]{2,1,0:T(8,128)S(1)}, f32[2,128,256]{2,1,0:T(8,128)S(1)}, u32[]{:S(2)}, u32[]{:S(2)}) collective-permute-start(f32[2,128,256]{2,1,0:T(8,128)S(1)} %get-tuple-element.140), channel_id=1, source_target_pairs={{0,16},{1,2},{2,1},{3,4},{4,3},{5,6},{6,5},{7,8},{8,7},{9,10},{10,... | collective-permute-start | bytes 786440 | tf_op jit(solution)/shard_map/ppermute | solution.py:303
  149.1 10.4 %collective-permute-start.21 = (f32[2,128,256]{2,1,0:T(8,128)S(1)}, f32[2,128,256]{2,1,0:T(8,128)S(1)}, u32[]{:S(2)}, u32[]{:S(2)}) collective-permute-start(f32[2,128,256]{2,1,0:T(8,128)S(1)} %get-tuple-element.138), channel_id=1, source_target_pairs={{0,16},{1,2},{2,1},{3,4},{4,3},{5,6},{6,5},{7,8},{8,7},{9,10},{10,... | collective-permute-start | bytes 786440 | tf_op jit(solution)/shard_map/ppermute | solution.py:303
  160.4 12.6 %collective-permute-start.24 = (f32[8,256]{1,0:T(8,128)S(1)}, f32[8,256]{1,0:T(8,128)S(1)}, u32[]{:S(2)}, u32[]{:S(2)}) collective-permute-start(f32[8,256]{1,0:T(8,128)S(1)} %get-tuple-element.149), channel_id=1, source_target_pairs={{0,1},{1,0},{2,3},{3,2},{4,5},{5,4},{6,7},{7,6},{8,9},{9,8},{10,11... | collective-permute-start | bytes 24584 | tf_op jit(solution)/shard_map/ppermute | solution.py:361
  (7 other events, 20.1 us)

commit v3 on v2

--- a/solution.py
+++ b/solution.py
@@ -193,6 +193,7 @@
             ready = done + [(ahead, weights.at[instant])]
             add_image((1 - odd) * EDGE, planes - EDGE, ready, sketches, before, image, light)
             add_image(odd * (planes - EDGE), EDGE, done, sketches, before, image, light)
+            send[...] = largest_light((1 - odd) * EDGE, planes - EDGE, light)
         else:
             add_image(0, planes, done, sketches, before, image, light)
 
@@ -250,16 +251,20 @@
     lax.fori_loop(0, count * down, body, 0, unroll=2)
 
 
-def last_body(planes, field, weights, sketches, image_in, light_in, image, light, most):
-    odd = lax.rem(lax.axis_index("gx"), 2)
-    add_image(odd * (planes - EDGE), EDGE, [(field, weights.at[weights.shape[0] - 1])], sketches,
-              (image_in, light_in), image, light)
+def largest_light(low, count, light):
     breadth, height = light.shape[1:]
 
     def highest(p):
         return jnp.max(light[p].reshape(breadth // 8, 8, height), axis=0)
 
-    most[...] = lax.fori_loop(1, planes, lambda p, so_far: jnp.maximum(so_far, highest(p)), highest(0))
+    return lax.fori_loop(1, count, lambda d, most: jnp.maximum(most, highest(low + d)), highest(low))
+
+
+def last_body(planes, field, weights, sketches, so_far, image_in, light_in, image, light, most):
+    odd = lax.rem(lax.axis_index("gx"), 2)
+    low = odd * (planes - EDGE)
+    add_image(low, EDGE, [(field, weights.at[weights.shape[0] - 1])], sketches, (image_in, light_in), image, light)
+    most[...] = jnp.maximum(so_far[...], largest_light(low, EDGE, light))
 
 
 def divide_body(planes, image, light, most, out, quotient, sems):
@@ -335,7 +340,7 @@
             inputs = [*tables, field, last, courant, weights, sketches, *images]
             ahead, near_sent, *images = call(
                 functools.partial(main_body, shots, planes, instant, closing),
-                (whole, both, still, still), [VMEM] * len(inputs),
+                (whole, held(8, height) if closing else both, still, still), [VMEM] * len(inputs),
                 aliases={len(inputs) - 2: 2, len(inputs) - 1: 3} if images else {},
                 flops=2 * planes * shots * breadth * height * 512, moved=8 * planes * shots * plane_bytes,
             )(*inputs)
@@ -353,9 +358,9 @@
         field, last = ahead, field
     image, light, most = call(
         functools.partial(last_body, planes),
-        (still, still, held(8, height)), [VMEM] * 5, aliases={3: 0, 4: 1},
+        (still, still, held(8, height)), [VMEM] * 6, aliases={4: 0, 5: 1},
         moved=8 * planes * shots * plane_bytes,
-    )(field, weights, sketches, *images)
+    )(field, weights, sketches, near_sent, *images)
     reach = 1
     while reach < count:
         most = jnp.maximum(most, lax.ppermute(most, "gx", [(i, i ^ reach) for i in range(count)]))

time: 187 us -> 186 us (level)
  no operation moved by 1% of the time
where the time goes in v3:
time: 186 us
  starting transfers between devices  66 us (35%)
  Pallas kernels  63.6 us (34%)
  waiting for transfers between devices  53.2 us (29%)
  local copies, waits for them, and re-layouts  2.11 us (1%)
    pallas_call x7, Pallas kernels, per_device(): call(functools.partial(main_body, shots, planes, instant, closing), (whol...  48 us
    ppermute x16, waiting for transfers between devices, to_far(): return lax.ppermute(planes_out, ('survey', 'gx'), far_pairs)  46.3 us
    ppermute x8, starting transfers between devices, to_near(): return lax.ppermute(planes_out, 'gx', near_pairs)  31.8 us
    ppermute x16, starting transfers between devices, to_far(): return lax.ppermute(planes_out, ('survey', 'gx'), far_pairs)  18 us
    ppermute x4, starting transfers between devices, per_device(): lax.ppermute(most, 'gx', [(i, i ^ reach) for i in range(count)])  16.2 us
    pallas_call x1, Pallas kernels, per_device(): call(functools.partial(main_body, shots, planes, 0, False), (whole, both,...  6.59 us
    ppermute x4, waiting for transfers between devices, per_device(): lax.ppermute(most, 'gx', [(i, i ^ reach) for i in range(count)])  6.29 us
    pallas_call x16, Pallas kernels, per_device(): call(functools.partial(far_body, instant, shot, planes), (whole,) if clos...  4.84 us
  transfers between devices with their start and end apart: 28, of which 18 were waited for; matrix products, arithmetic and copies ran while one was open for 1% of the time, Pallas kernels for 7%

profile of v3, /device:TPU:0, one launch (start us, length us, event | category | flops | bytes accessed | tf_op | source)
XLA Modules:
  0.0 186.0 jit_solution(11742215045331820634)
XLA Ops:
  4.1 6.6 %shard_map.88 = (f32[2,16,128,256]{3,2,1,0:T(8,128)S(1)}, f32[4,128,256]{2,1,0:T(8,128)S(1)}, f32[2,16,128,256]{3,2,1,0:T(8,128)S(1)}, f32[2,16,128,256]{3,2,1,0...) custom-call(bf16[256,256]{1,0:T(8,128)(2,1)S(1)} %get-tuple-element.77.refs_0_.along_z, ...), custom_call_target="tpu_custom_call" | custom-call | flops 1073741824 | bytes 33554432 | tf_op jit(solution)/shard_map/pallas_call | solution.py:333
  13.8 4.3 %collective-permute-done.2.ghost = f32[2,128,256]{2,1,0:T(8,128)S(1)} collective-permute-done((f32[2,128,256]{2,1,0:T(8,128)S(1)}, f32[2,128,256]{2,1,0:T(8,128)S(1)}, u32[]{:S(2)}, u32[]{:S(2)}) %collective-permute-start.2) | collective-permute-done | bytes 262176 | tf_op jit(solution)/shard_map/ppermute | solution.py:308
  21.3 6.6 %shard_map.91 = (f32[2,16,128,256]{3,2,1,0:T(8,128)S(1)}, f32[4,128,256]{2,1,0:T(8,128)S(1)}, f32[16,128,256]{2,1,0:T(8,128)S(1)}, f32[16,128,256]{2,1,0:T(8,128)S(1)}) custom-call(bf16[256,256]{1,0:T(8,128)(2,1)S(1)} %get-tuple-element.77.refs_0_.along_z, bf16[128,256]{1,0:T(8,128)(2,1)S(1)} %get-tuple-element.78.refs_1_.along_y, ...), custom_call_target="tpu_custom_call" | custom-call | flops 1073741824 | bytes 33554432 | tf_op jit(solution)/shard_map/pallas_call | solution.py:341
  27.9 4.8 %collective-permute-start.8 = (f32[4,128,256]{2,1,0:T(8,128)S(1)}, f32[4,128,256]{2,1,0:T(8,128)S(1)}, u32[]{:S(2)}, u32[]{:S(2)}) collective-permute-start(f32[4,128,256]{2,1,0:T(8,128)S(1)} %get-tuple-element.102), channel_id=1, source_target_pairs={{0,1},{1,0},{2,3},{3,2},{4,5},{5,4},{6,7},{7,6},{8,9},{9,8},{10,11... | collective-permute-start | bytes 1572872 | tf_op jit(solution)/shard_map/ppermute | solution.py:311
  34.7 4.3 %collective-permute-done.4.ghost = f32[2,128,256]{2,1,0:T(8,128)S(1)} collective-permute-done((f32[2,128,256]{2,1,0:T(8,128)S(1)}, f32[2,128,256]{2,1,0:T(8,128)S(1)}, u32[]{:S(2)}, u32[]{:S(2)}) %collective-permute-start.4) | collective-permute-done | bytes 262176 | tf_op jit(solution)/shard_map/ppermute | solution.py:308
  42.2 6.6 %shard_map.94 = (f32[2,16,128,256]{3,2,1,0:T(8,128)S(1)}, f32[4,128,256]{2,1,0:T(8,128)S(1)}, f32[16,128,256]{2,1,0:T(8,128)S(1)}, f32[16,128,256]{2,1,0:T(8,128)S(1)}) custom-call(bf16[256,256]{1,0:T(8,128)(2,1)S(1)} %get-tuple-element.77.refs_0_.along_z, ...), custom_call_target="tpu_custom_call", output_to_operand_aliasing={{2}: (11, {}), {3}: (12, {})} | custom-call | flops 1073741824 | bytes 33554432 | tf_op jit(solution)/shard_map/pallas_call | solution.py:341
  48.8 5.2 %collective-permute-start.11 = (f32[4,128,256]{2,1,0:T(8,128)S(1)}, f32[4,128,256]{2,1,0:T(8,128)S(1)}, u32[]{:S(2)}, u32[]{:S(2)}) collective-permute-start(f32[4,128,256]{2,1,0:T(8,128)S(1)} %get-tuple-element.110), channel_id=1, source_target_pairs={{0,1},{1,0},{2,3},{3,2},{4,5},{5,4},{6,7},{7,6},{8,9},{9,8},{10,11... | collective-permute-start | bytes 1572872 | tf_op jit(solution)/shard_map/ppermute | solution.py:311
  56.0 4.3 %collective-permute-done.7.ghost = f32[2,128,256]{2,1,0:T(8,128)S(1)} collective-permute-done((f32[2,128,256]{2,1,0:T(8,128)S(1)}, f32[2,128,256]{2,1,0:T(8,128)S(1)}, u32[]{:S(2)}, u32[]{:S(2)}) %collective-permute-start.7) | collective-permute-done | bytes 262176 | tf_op jit(solution)/shard_map/ppermute | solution.py:308
  63.5 6.6 %shard_map.97 = (f32[2,16,128,256]{3,2,1,0:T(8,128)S(1)}, f32[4,128,256]{2,1,0:T(8,128)S(1)}, f32[16,128,256]{2,1,0:T(8,128)S(1)}, f32[16,128,256]{2,1,0:T(8,128)S(1)}) custom-call(bf16[256,256]{1,0:T(8,128)(2,1)S(1)} %get-tuple-element.77.refs_0_.along_z, ...), custom_call_target="tpu_custom_call", output_to_operand_aliasing={{2}: (11, {}), {3}: (12, {})} | custom-call | flops 1073741824 | bytes 33554432 | tf_op jit(solution)/shard_map/pallas_call | solution.py:341
  70.2 5.2 %collective-permute-start.14 = (f32[4,128,256]{2,1,0:T(8,128)S(1)}, f32[4,128,256]{2,1,0:T(8,128)S(1)}, u32[]{:S(2)}, u32[]{:S(2)}) collective-permute-start(f32[4,128,256]{2,1,0:T(8,128)S(1)} %get-tuple-element.118), channel_id=1, source_target_pairs={{0,1},{1,0},{2,3},{3,2},{4,5},{5,4},{6,7},{7,6},{8,9},{9,8},{10,11... | collective-permute-start | bytes 1572872 | tf_op jit(solution)/shard_map/ppermute | solution.py:311
  77.4 4.3 %collective-permute-done.10.ghost = f32[2,128,256]{2,1,0:T(8,128)S(1)} collective-permute-done((f32[2,128,256]{2,1,0:T(8,128)S(1)}, f32[2,128,256]{2,1,0:T(8,128)S(1)}, u32[]{:S(2)}, u32[]{:S(2)}) %collective-permute-start.10) | collective-permute-done | bytes 262176 | tf_op jit(solution)/shard_map/ppermute | solution.py:308
  84.9 6.6 %shard_map.100 = (f32[2,16,128,256]{3,2,1,0:T(8,128)S(1)}, f32[4,128,256]{2,1,0:T(8,128)S(1)}, f32[16,128,256]{2,1,0:T(8,128)S(1)}, f32[16,128,256]{2,1,0:T(8,128)S(1)}) custom-call(bf16[256,256]{1,0:T(8,128)(2,1)S(1)} %get-tuple-element.77.refs_0_.along_z, ...), custom_call_target="tpu_custom_call", output_to_operand_aliasing={{2}: (11, {}), {3}: (12, {})} | custom-call | flops 1073741824 | bytes 33554432 | tf_op jit(solution)/shard_map/pallas_call | solution.py:341
  91.5 5.2 %collective-permute-start.17 = (f32[4,128,256]{2,1,0:T(8,128)S(1)}, f32[4,128,256]{2,1,0:T(8,128)S(1)}, u32[]{:S(2)}, u32[]{:S(2)}) collective-permute-start(f32[4,128,256]{2,1,0:T(8,128)S(1)} %get-tuple-element.126), channel_id=1, source_target_pairs={{0,1},{1,0},{2,3},{3,2},{4,5},{5,4},{6,7},{7,6},{8,9},{9,8},{10,11... | collective-permute-start | bytes 1572872 | tf_op jit(solution)/shard_map/ppermute | solution.py:311
  98.8 4.3 %collective-permute-done.13.ghost = f32[2,128,256]{2,1,0:T(8,128)S(1)} collective-permute-done((f32[2,128,256]{2,1,0:T(8,128)S(1)}, f32[2,128,256]{2,1,0:T(8,128)S(1)}, u32[]{:S(2)}, u32[]{:S(2)}) %collective-permute-start.13) | collective-permute-done | bytes 262176 | tf_op jit(solution)/shard_map/ppermute | solution.py:308
  106.2 6.8 %shard_map.103 = (f32[2,16,128,256]{3,2,1,0:T(8,128)S(1)}, f32[4,128,256]{2,1,0:T(8,128)S(1)}, f32[16,128,256]{2,1,0:T(8,128)S(1)}, f32[16,128,256]{2,1,0:T(8,128)S(1)}) custom-call(bf16[256,256]{1,0:T(8,128)(2,1)S(1)} %get-tuple-element.77.refs_0_.along_z, ...), custom_call_target="tpu_custom_call", output_to_operand_aliasing={{2}: (11, {}), {3}: (12, {})} | custom-call | flops 1073741824 | bytes 33554432 | tf_op jit(solution)/shard_map/pallas_call | solution.py:341
  113.1 5.2 %collective-permute-start.20 = (f32[4,128,256]{2,1,0:T(8,128)S(1)}, f32[4,128,256]{2,1,0:T(8,128)S(1)}, u32[]{:S(2)}, u32[]{:S(2)}) collective-permute-start(f32[4,128,256]{2,1,0:T(8,128)S(1)} %get-tuple-element.134), channel_id=1, source_target_pairs={{0,1},{1,0},{2,3},{3,2},{4,5},{5,4},{6,7},{7,6},{8,9},{9,8},{10,11... | collective-permute-start | bytes 1572872 | tf_op jit(solution)/shard_map/ppermute | solution.py:311
  120.3 4.3 %collective-permute-done.16.ghost = f32[2,128,256]{2,1,0:T(8,128)S(1)} collective-permute-done((f32[2,128,256]{2,1,0:T(8,128)S(1)}, f32[2,128,256]{2,1,0:T(8,128)S(1)}, u32[]{:S(2)}, u32[]{:S(2)}) %collective-permute-start.16) | collective-permute-done | bytes 262176 | tf_op jit(solution)/shard_map/ppermute | solution.py:308
  127.8 6.6 %shard_map.106 = (f32[2,16,128,256]{3,2,1,0:T(8,128)S(1)}, f32[4,128,256]{2,1,0:T(8,128)S(1)}, f32[16,128,256]{2,1,0:T(8,128)S(1)}, f32[16,128,256]{2,1,0:T(8,128)S(1)}) custom-call(bf16[256,256]{1,0:T(8,128)(2,1)S(1)} %get-tuple-element.77.refs_0_.along_z, ...), custom_call_target="tpu_custom_call", output_to_operand_aliasing={{2}: (11, {}), {3}: (12, {})} | custom-call | flops 1073741824 | bytes 33554432 | tf_op jit(solution)/shard_map/pallas_call | solution.py:341
  134.4 5.2 %collective-permute-start.23 = (f32[4,128,256]{2,1,0:T(8,128)S(1)}, f32[4,128,256]{2,1,0:T(8,128)S(1)}, u32[]{:S(2)}, u32[]{:S(2)}) collective-permute-start(f32[4,128,256]{2,1,0:T(8,128)S(1)} %get-tuple-element.142), channel_id=1, source_target_pairs={{0,1},{1,0},{2,3},{3,2},{4,5},{5,4},{6,7},{7,6},{8,9},{9,8},{10,11... | collective-permute-start | bytes 1572872 | tf_op jit(solution)/shard_map/ppermute | solution.py:311
  141.7 4.3 %collective-permute-done.19.ghost = f32[2,128,256]{2,1,0:T(8,128)S(1)} collective-permute-done((f32[2,128,256]{2,1,0:T(8,128)S(1)}, f32[2,128,256]{2,1,0:T(8,128)S(1)}, u32[]{:S(2)}, u32[]{:S(2)}) %collective-permute-start.19) | collective-permute-done | bytes 262176 | tf_op jit(solution)/shard_map/ppermute | solution.py:308
  150.7 7.9 %shard_map.109 = (f32[2,16,128,256]{3,2,1,0:T(8,128)S(1)}, f32[8,256]{1,0:T(8,128)S(1)}, f32[16,128,256]{2,1,0:T(8,128)S(1)}, f32[16,128,256]{2,1,0:T(8,128)S(1)}) custom-call(bf16[256,256]{1,0:T(8,128)(2,1)S(1)} %get-tuple-element.77.refs_0_.along_z, ...), custom_call_target="tpu_custom_call", output_to_operand_aliasing={{2}: (11, {}), {3}: (12, {})} | custom-call | flops 1073741824 | bytes 33554432 | tf_op jit(solution)/shard_map/pallas_call | solution.py:341
  159.7 11.8 %collective-permute-start.24 = (f32[8,256]{1,0:T(8,128)S(1)}, f32[8,256]{1,0:T(8,128)S(1)}, u32[]{:S(2)}, u32[]{:S(2)}) collective-permute-start(f32[8,256]{1,0:T(8,128)S(1)} %get-tuple-element.151), channel_id=1, source_target_pairs={{0,1},{1,0},{2,3},{3,2},{4,5},{5,4},{6,7},{7,6},{8,9},{9,8},{10,11... | collective-permute-start | bytes 24584 | tf_op jit(solution)/shard_map/ppermute | solution.py:366
  172.5 3.4 %collective-permute-done.25 = f32[8,256]{1,0:T(8,128)S(1)} collective-permute-done((f32[8,256]{1,0:T(8,128)S(1)}, f32[8,256]{1,0:T(8,128)S(1)}, u32[]{:S(2)}, u32[]{:S(2)}) %collective-permute-start.25) | collective-permute-done | bytes 8224 | tf_op jit(solution)/shard_map/ppermute | solution.py:366
  179.6 2.6 %collective-permute-start.27 = (f32[8,256]{1,0:T(8,128)S(1)}, f32[8,256]{1,0:T(8,128)S(1)}, u32[]{:S(2)}, u32[]{:S(2)}) collective-permute-start(f32[8,256]{1,0:T(8,128)S(1)} %max.14), channel_id=1, source_target_pairs={{0,8},{1,9},{2,10},{3,11},{4,12},{5,13},{6,14},{7,15},{8,0},{9,1},... | collective-permute-start | bytes 24584 | tf_op jit(solution)/shard_map/ppermute | solution.py:366
  (72 shorter events, 51.3 us)
Async XLA Ops:
  10.7 10.5 %collective-permute-start.5 = (f32[4,128,256]{2,1,0:T(8,128)S(1)}, f32[4,128,256]{2,1,0:T(8,128)S(1)}, u32[]{:S(2)}, u32[]{:S(2)}) collective-permute-start(f32[4,128,256]{2,1,0:T(8,128)S(1)} %get-tuple-element.94), channel_id=1, source_target_pairs={{0,1},{1,0},{2,3},{3,2},{4,5},{5,4},{6,7},{7,6},{8,9},{9,8},{10,11... | collective-permute-start | bytes 1572872 | tf_op jit(solution)/shard_map/ppermute | solution.py:311
  11.2 7.0 %collective-permute-start.2 = (f32[2,128,256]{2,1,0:T(8,128)S(1)}, f32[2,128,256]{2,1,0:T(8,128)S(1)}, u32[]{:S(2)}, u32[]{:S(2)}) collective-permute-start(f32[2,128,256]{2,1,0:T(8,128)S(1)} %get-tuple-element.88), channel_id=1, source_target_pairs={{0,16},{1,2},{2,1},{3,4},{4,3},{5,6},{6,5},{7,8},{8,7},{9,10},{10,... | collective-permute-start | bytes 786440 | tf_op jit(solution)/shard_map/ppermute | solution.py:308
  13.8 7.2 %collective-permute-start = (f32[2,128,256]{2,1,0:T(8,128)S(1)}, f32[2,128,256]{2,1,0:T(8,128)S(1)}, u32[]{:S(2)}, u32[]{:S(2)}) collective-permute-start(f32[2,128,256]{2,1,0:T(8,128)S(1)} %get-tuple-element.81), channel_id=1, source_target_pairs={{0,16},{1,2},{2,1},{3,4},{4,3},{5,6},{6,5},{7,8},{8,7},{9,10},{10,... | collective-permute-start | bytes 786440 | tf_op jit(solution)/shard_map/ppermute | solution.py:308
  27.9 14.3 %collective-permute-start.8 = (f32[4,128,256]{2,1,0:T(8,128)S(1)}, f32[4,128,256]{2,1,0:T(8,128)S(1)}, u32[]{:S(2)}, u32[]{:S(2)}) collective-permute-start(f32[4,128,256]{2,1,0:T(8,128)S(1)} %get-tuple-element.102), channel_id=1, source_target_pairs={{0,1},{1,0},{2,3},{3,2},{4,5},{5,4},{6,7},{7,6},{8,9},{9,8},{10,11... | collective-permute-start | bytes 1572872 | tf_op jit(solution)/shard_map/ppermute | solution.py:311
  32.7 6.4 %collective-permute-start.4 = (f32[2,128,256]{2,1,0:T(8,128)S(1)}, f32[2,128,256]{2,1,0:T(8,128)S(1)}, u32[]{:S(2)}, u32[]{:S(2)}) collective-permute-start(f32[2,128,256]{2,1,0:T(8,128)S(1)} %get-tuple-element.93), channel_id=1, source_target_pairs={{0,16},{1,2},{2,1},{3,4},{4,3},{5,6},{6,5},{7,8},{8,7},{9,10},{10,... | collective-permute-start | bytes 786440 | tf_op jit(solution)/shard_map/ppermute | solution.py:308
  34.2 7.7 %collective-permute-start.3 = (f32[2,128,256]{2,1,0:T(8,128)S(1)}, f32[2,128,256]{2,1,0:T(8,128)S(1)}, u32[]{:S(2)}, u32[]{:S(2)}) collective-permute-start(f32[2,128,256]{2,1,0:T(8,128)S(1)} %get-tuple-element.91), channel_id=1, source_target_pairs={{0,16},{1,2},{2,1},{3,4},{4,3},{5,6},{6,5},{7,8},{8,7},{9,10},{10,... | collective-permute-start | bytes 786440 | tf_op jit(solution)/shard_map/ppermute | solution.py:308
  48.8 14.7 %collective-permute-start.11 = (f32[4,128,256]{2,1,0:T(8,128)S(1)}, f32[4,128,256]{2,1,0:T(8,128)S(1)}, u32[]{:S(2)}, u32[]{:S(2)}) collective-permute-start(f32[4,128,256]{2,1,0:T(8,128)S(1)} %get-tuple-element.110), channel_id=1, source_target_pairs={{0,1},{1,0},{2,3},{3,2},{4,5},{5,4},{6,7},{7,6},{8,9},{9,8},{10,11... | collective-permute-start | bytes 1572872 | tf_op jit(solution)/shard_map/ppermute | solution.py:311
  54.0 6.4 %collective-permute-start.7 = (f32[2,128,256]{2,1,0:T(8,128)S(1)}, f32[2,128,256]{2,1,0:T(8,128)S(1)}, u32[]{:S(2)}, u32[]{:S(2)}) collective-permute-start(f32[2,128,256]{2,1,0:T(8,128)S(1)} %get-tuple-element.101), channel_id=1, source_target_pairs={{0,16},{1,2},{2,1},{3,4},{4,3},{5,6},{6,5},{7,8},{8,7},{9,10},{10,... | collective-permute-start | bytes 786440 | tf_op jit(solution)/shard_map/ppermute | solution.py:308
  55.5 7.7 %collective-permute-start.6 = (f32[2,128,256]{2,1,0:T(8,128)S(1)}, f32[2,128,256]{2,1,0:T(8,128)S(1)}, u32[]{:S(2)}, u32[]{:S(2)}) collective-permute-start(f32[2,128,256]{2,1,0:T(8,128)S(1)} %get-tuple-element.99), channel_id=1, source_target_pairs={{0,16},{1,2},{2,1},{3,4},{4,3},{5,6},{6,5},{7,8},{8,7},{9,10},{10,... | collective-permute-start | bytes 786440 | tf_op jit(solution)/shard_map/ppermute | solution.py:308
  70.2 14.7 %collective-permute-start.14 = (f32[4,128,256]{2,1,0:T(8,128)S(1)}, f32[4,128,256]{2,1,0:T(8,128)S(1)}, u32[]{:S(2)}, u32[]{:S(2)}) collective-permute-start(f32[4,128,256]{2,1,0:T(8,128)S(1)} %get-tuple-element.118), channel_id=1, source_target_pairs={{0,1},{1,0},{2,3},{3,2},{4,5},{5,4},{6,7},{7,6},{8,9},{9,8},{10,11... | collective-permute-start | bytes 1572872 | tf_op jit(solution)/shard_map/ppermute | solution.py:311
  75.4 6.4 %collective-permute-start.10 = (f32[2,128,256]{2,1,0:T(8,128)S(1)}, f32[2,128,256]{2,1,0:T(8,128)S(1)}, u32[]{:S(2)}, u32[]{:S(2)}) collective-permute-start(f32[2,128,256]{2,1,0:T(8,128)S(1)} %get-tuple-element.109), channel_id=1, source_target_pairs={{0,16},{1,2},{2,1},{3,4},{4,3},{5,6},{6,5},{7,8},{8,7},{9,10},{10,... | collective-permute-start | bytes 786440 | tf_op jit(solution)/shard_map/ppermute | solution.py:308
  76.9 7.7 %collective-permute-start.9 = (f32[2,128,256]{2,1,0:T(8,128)S(1)}, f32[2,128,256]{2,1,0:T(8,128)S(1)}, u32[]{:S(2)}, u32[]{:S(2)}) collective-permute-start(f32[2,128,256]{2,1,0:T(8,128)S(1)} %get-tuple-element.107), channel_id=1, source_target_pairs={{0,16},{1,2},{2,1},{3,4},{4,3},{5,6},{6,5},{7,8},{8,7},{9,10},{10,... | collective-permute-start | bytes 786440 | tf_op jit(solution)/shard_map/ppermute | solution.py:308
  91.5 14.7 %collective-permute-start.17 = (f32[4,128,256]{2,1,0:T(8,128)S(1)}, f32[4,128,256]{2,1,0:T(8,128)S(1)}, u32[]{:S(2)}, u32[]{:S(2)}) collective-permute-start(f32[4,128,256]{2,1,0:T(8,128)S(1)} %get-tuple-element.126), channel_id=1, source_target_pairs={{0,1},{1,0},{2,3},{3,2},{4,5},{5,4},{6,7},{7,6},{8,9},{9,8},{10,11... | collective-permute-start | bytes 1572872 | tf_op jit(solution)/shard_map/ppermute | solution.py:311
  96.7 6.4 %collective-permute-start.13 = (f32[2,128,256]{2,1,0:T(8,128)S(1)}, f32[2,128,256]{2,1,0:T(8,128)S(1)}, u32[]{:S(2)}, u32[]{:S(2)}) collective-permute-start(f32[2,128,256]{2,1,0:T(8,128)S(1)} %get-tuple-element.117), channel_id=1, source_target_pairs={{0,16},{1,2},{2,1},{3,4},{4,3},{5,6},{6,5},{7,8},{8,7},{9,10},{10,... | collective-permute-start | bytes 786440 | tf_op jit(solution)/shard_map/ppermute | solution.py:308
  98.2 7.7 %collective-permute-start.12 = (f32[2,128,256]{2,1,0:T(8,128)S(1)}, f32[2,128,256]{2,1,0:T(8,128)S(1)}, u32[]{:S(2)}, u32[]{:S(2)}) collective-permute-start(f32[2,128,256]{2,1,0:T(8,128)S(1)} %get-tuple-element.115), channel_id=1, source_target_pairs={{0,16},{1,2},{2,1},{3,4},{4,3},{5,6},{6,5},{7,8},{8,7},{9,10},{10,... | collective-permute-start | bytes 786440 | tf_op jit(solution)/shard_map/ppermute | solution.py:308
  113.1 14.7 %collective-permute-start.20 = (f32[4,128,256]{2,1,0:T(8,128)S(1)}, f32[4,128,256]{2,1,0:T(8,128)S(1)}, u32[]{:S(2)}, u32[]{:S(2)}) collective-permute-start(f32[4,128,256]{2,1,0:T(8,128)S(1)} %get-tuple-element.134), channel_id=1, source_target_pairs={{0,1},{1,0},{2,3},{3,2},{4,5},{5,4},{6,7},{7,6},{8,9},{9,8},{10,11... | collective-permute-start | bytes 1572872 | tf_op jit(solution)/shard_map/ppermute | solution.py:311
  118.3 6.4 %collective-permute-start.16 = (f32[2,128,256]{2,1,0:T(8,128)S(1)}, f32[2,128,256]{2,1,0:T(8,128)S(1)}, u32[]{:S(2)}, u32[]{:S(2)}) collective-permute-start(f32[2,128,256]{2,1,0:T(8,128)S(1)} %get-tuple-element.125), channel_id=1, source_target_pairs={{0,16},{1,2},{2,1},{3,4},{4,3},{5,6},{6,5},{7,8},{8,7},{9,10},{10,... | collective-permute-start | bytes 786440 | tf_op jit(solution)/shard_map/ppermute | solution.py:308
  119.8 7.7 %collective-permute-start.15 = (f32[2,128,256]{2,1,0:T(8,128)S(1)}, f32[2,128,256]{2,1,0:T(8,128)S(1)}, u32[]{:S(2)}, u32[]{:S(2)}) collective-permute-start(f32[2,128,256]{2,1,0:T(8,128)S(1)} %get-tuple-element.123), channel_id=1, source_target_pairs={{0,16},{1,2},{2,1},{3,4},{4,3},{5,6},{6,5},{7,8},{8,7},{9,10},{10,... | collective-permute-start | bytes 786440 | tf_op jit(solution)/shard_map/ppermute | solution.py:308
  134.4 16.3 %collective-permute-start.23 = (f32[4,128,256]{2,1,0:T(8,128)S(1)}, f32[4,128,256]{2,1,0:T(8,128)S(1)}, u32[]{:S(2)}, u32[]{:S(2)}) collective-permute-start(f32[4,128,256]{2,1,0:T(8,128)S(1)} %get-tuple-element.142), channel_id=1, source_target_pairs={{0,1},{1,0},{2,3},{3,2},{4,5},{5,4},{6,7},{7,6},{8,9},{9,8},{10,11... | collective-permute-start | bytes 1572872 | tf_op jit(solution)/shard_map/ppermute | solution.py:311
  139.6 6.4 %collective-permute-start.19 = (f32[2,128,256]{2,1,0:T(8,128)S(1)}, f32[2,128,256]{2,1,0:T(8,128)S(1)}, u32[]{:S(2)}, u32[]{:S(2)}) collective-permute-start(f32[2,128,256]{2,1,0:T(8,128)S(1)} %get-tuple-element.133), channel_id=1, source_target_pairs={{0,16},{1,2},{2,1},{3,4},{4,3},{5,6},{6,5},{7,8},{8,7},{9,10},{10,... | collective-permute-start | bytes 786440 | tf_op jit(solution)/shard_map/ppermute | solution.py:308
  141.2 7.7 %collective-permute-start.18 = (f32[2,128,256]{2,1,0:T(8,128)S(1)}, f32[2,128,256]{2,1,0:T(8,128)S(1)}, u32[]{:S(2)}, u32[]{:S(2)}) collective-permute-start(f32[2,128,256]{2,1,0:T(8,128)S(1)} %get-tuple-element.131), channel_id=1, source_target_pairs={{0,16},{1,2},{2,1},{3,4},{4,3},{5,6},{6,5},{7,8},{8,7},{9,10},{10,... | collective-permute-start | bytes 786440 | tf_op jit(solution)/shard_map/ppermute | solution.py:308
  146.3 12.3 %collective-permute-start.22 = (f32[2,128,256]{2,1,0:T(8,128)S(1)}, f32[2,128,256]{2,1,0:T(8,128)S(1)}, u32[]{:S(2)}, u32[]{:S(2)}) collective-permute-start(f32[2,128,256]{2,1,0:T(8,128)S(1)} %get-tuple-element.141), channel_id=1, source_target_pairs={{0,16},{1,2},{2,1},{3,4},{4,3},{5,6},{6,5},{7,8},{8,7},{9,10},{10,... | collective-permute-start | bytes 786440 | tf_op jit(solution)/shard_map/ppermute | solution.py:308
  149.1 9.8 %collective-permute-start.21 = (f32[2,128,256]{2,1,0:T(8,128)S(1)}, f32[2,128,256]{2,1,0:T(8,128)S(1)}, u32[]{:S(2)}, u32[]{:S(2)}) collective-permute-start(f32[2,128,256]{2,1,0:T(8,128)S(1)} %get-tuple-element.139), channel_id=1, source_target_pairs={{0,16},{1,2},{2,1},{3,4},{4,3},{5,6},{6,5},{7,8},{8,7},{9,10},{10,... | collective-permute-start | bytes 786440 | tf_op jit(solution)/shard_map/ppermute | solution.py:308
  159.7 12.6 %collective-permute-start.24 = (f32[8,256]{1,0:T(8,128)S(1)}, f32[8,256]{1,0:T(8,128)S(1)}, u32[]{:S(2)}, u32[]{:S(2)}) collective-permute-start(f32[8,256]{1,0:T(8,128)S(1)} %get-tuple-element.151), channel_id=1, source_target_pairs={{0,1},{1,0},{2,3},{3,2},{4,5},{5,4},{6,7},{7,6},{8,9},{9,8},{10,11... | collective-permute-start | bytes 24584 | tf_op jit(solution)/shard_map/ppermute | solution.py:366
  (7 other events, 20.1 us)

commit v4 on v3

--- a/solution.py
+++ b/solution.py
@@ -13,6 +13,7 @@
 SMEM = pl.BlockSpec(memory_space=pltpu.SMEM)
 ANY = pl.BlockSpec(memory_space=pl.ANY)
 EDGE = 2
+WRITES = 8
 CHUNKS = 4
 
 
@@ -171,7 +172,7 @@
     else:
         for j in range(EDGE):
             step(j)
-        lax.fori_loop(EDGE, planes - EDGE, body, 0, unroll=2)
+        lax.fori_loop(EDGE, planes - EDGE, body, 0, unroll=4)
     for s in range(shots):
         own = jnp.max(spot_plane[s]).astype(jnp.int32)
 
@@ -248,7 +249,7 @@
             light_out[p, row, column] = light.reshape(rows, columns)
         return carry
 
-    lax.fori_loop(0, count * down, body, 0, unroll=2)
+    lax.fori_loop(0, count * down, body, 0, unroll=4)
 
 
 def largest_light(low, count, light):
@@ -269,9 +270,9 @@
 
 def divide_body(planes, image, light, most, out, quotient, sems):
     largest = 0.1 * jnp.max(most[...])
-    slab = planes // CHUNKS
+    slab = planes // WRITES
     copies = []
-    for c in range(CHUNKS):
+    for c in range(WRITES):
         def body(p, carry):
             quotient[p] = image[p] / (light[p] + largest)
             return carry
@@ -367,7 +368,7 @@
         reach *= 2
     result = call(
         functools.partial(divide_body, planes), pltpu.HBM((planes, breadth, height), F32), [VMEM] * 3,
-        scratch=[pltpu.VMEM((planes, breadth, height), F32), pltpu.SemaphoreType.DMA((CHUNKS,))], out_spec=ANY,
+        scratch=[pltpu.VMEM((planes, breadth, height), F32), pltpu.SemaphoreType.DMA((WRITES,))], out_spec=ANY,
         moved=3 * planes * plane_bytes,
     )(image, light, most)
     return result, field

time: 186 us -> 181 us (0.973)
  Pallas kernels: 63.6 us -> 58.2 us
    pallas_call x7, Pallas kernels: 48 us -> 42.7 us  [per_device(): call(functools.partial(main_body, shots, planes, instant, closing), (whol...]
where the time goes in v4:
time: 181 us
  starting transfers between devices  65.9 us (36%)
  Pallas kernels  58.2 us (32%)
  waiting for transfers between devices  53.2 us (29%)
  local copies, waits for them, and re-layouts  2.11 us (1%)
    ppermute x16, waiting for transfers between devices, to_far(): return lax.ppermute(planes_out, ('survey', 'gx'), far_pairs)  46.3 us
    pallas_call x7, Pallas kernels, per_device(): call(functools.partial(main_body, shots, planes, instant, closing), (whol...  42.7 us
    ppermute x8, starting transfers between devices, to_near(): return lax.ppermute(planes_out, 'gx', near_pairs)  31.7 us
    ppermute x16, starting transfers between devices, to_far(): return lax.ppermute(planes_out, ('survey', 'gx'), far_pairs)  18 us
    ppermute x4, starting transfers between devices, per_device(): lax.ppermute(most, 'gx', [(i, i ^ reach) for i in range(count)])  16.2 us
    pallas_call x1, Pallas kernels, per_device(): call(functools.partial(main_body, shots, planes, 0, False), (whole, both,...  6.59 us
    ppermute x4, waiting for transfers between devices, per_device(): lax.ppermute(most, 'gx', [(i, i ^ reach) for i in range(count)])  6.29 us
    pallas_call x16, Pallas kernels, per_device(): call(functools.partial(far_body, instant, shot, planes), (whole,) if clos...  4.82 us
  transfers between devices with their start and end apart: 28, of which 18 were waited for; matrix products, arithmetic and copies ran while one was open for 1% of the time, Pallas kernels for 7%

profile of v4, /device:TPU:0, one launch (start us, length us, event | category | flops | bytes accessed | tf_op | source)
XLA Modules:
  0.0 180.5 jit_solution(17817256754347434949)
XLA Ops:
  4.1 6.6 %shard_map.88 = (f32[2,16,128,256]{3,2,1,0:T(8,128)S(1)}, f32[4,128,256]{2,1,0:T(8,128)S(1)}, f32[2,16,128,256]{3,2,1,0:T(8,128)S(1)}, f32[2,16,128,256]{3,2,1,0...) custom-call(bf16[256,256]{1,0:T(8,128)(2,1)S(1)} %get-tuple-element.77.refs_0_.along_z, ...), custom_call_target="tpu_custom_call" | custom-call | flops 1073741824 | bytes 33554432 | tf_op jit(solution)/shard_map/pallas_call | solution.py:334
  13.8 4.3 %collective-permute-done.2.ghost = f32[2,128,256]{2,1,0:T(8,128)S(1)} collective-permute-done((f32[2,128,256]{2,1,0:T(8,128)S(1)}, f32[2,128,256]{2,1,0:T(8,128)S(1)}, u32[]{:S(2)}, u32[]{:S(2)}) %collective-permute-start.2) | collective-permute-done | bytes 262176 | tf_op jit(solution)/shard_map/ppermute | solution.py:309
  21.3 5.7 %shard_map.91 = (f32[2,16,128,256]{3,2,1,0:T(8,128)S(1)}, f32[4,128,256]{2,1,0:T(8,128)S(1)}, f32[16,128,256]{2,1,0:T(8,128)S(1)}, f32[16,128,256]{2,1,0:T(8,128)S(1)}) custom-call(bf16[256,256]{1,0:T(8,128)(2,1)S(1)} %get-tuple-element.77.refs_0_.along_z, bf16[128,256]{1,0:T(8,128)(2,1)S(1)} %get-tuple-element.78.refs_1_.along_y, ...), custom_call_target="tpu_custom_call" | custom-call | flops 1073741824 | bytes 33554432 | tf_op jit(solution)/shard_map/pallas_call | solution.py:342
  26.9 4.8 %collective-permute-start.8 = (f32[4,128,256]{2,1,0:T(8,128)S(1)}, f32[4,128,256]{2,1,0:T(8,128)S(1)}, u32[]{:S(2)}, u32[]{:S(2)}) collective-permute-start(f32[4,128,256]{2,1,0:T(8,128)S(1)} %get-tuple-element.102), channel_id=1, source_target_pairs={{0,1},{1,0},{2,3},{3,2},{4,5},{5,4},{6,7},{7,6},{8,9},{9,8},{10,11... | collective-permute-start | bytes 1572872 | tf_op jit(solution)/shard_map/ppermute | solution.py:312
  33.7 4.3 %collective-permute-done.4.ghost = f32[2,128,256]{2,1,0:T(8,128)S(1)} collective-permute-done((f32[2,128,256]{2,1,0:T(8,128)S(1)}, f32[2,128,256]{2,1,0:T(8,128)S(1)}, u32[]{:S(2)}, u32[]{:S(2)}) %collective-permute-start.4) | collective-permute-done | bytes 262176 | tf_op jit(solution)/shard_map/ppermute | solution.py:309
  41.2 5.9 %shard_map.94 = (f32[2,16,128,256]{3,2,1,0:T(8,128)S(1)}, f32[4,128,256]{2,1,0:T(8,128)S(1)}, f32[16,128,256]{2,1,0:T(8,128)S(1)}, f32[16,128,256]{2,1,0:T(8,128)S(1)}) custom-call(bf16[256,256]{1,0:T(8,128)(2,1)S(1)} %get-tuple-element.77.refs_0_.along_z, ...), custom_call_target="tpu_custom_call", output_to_operand_aliasing={{2}: (11, {}), {3}: (12, {})} | custom-call | flops 1073741824 | bytes 33554432 | tf_op jit(solution)/shard_map/pallas_call | solution.py:342
  47.1 5.2 %collective-permute-start.11 = (f32[4,128,256]{2,1,0:T(8,128)S(1)}, f32[4,128,256]{2,1,0:T(8,128)S(1)}, u32[]{:S(2)}, u32[]{:S(2)}) collective-permute-start(f32[4,128,256]{2,1,0:T(8,128)S(1)} %get-tuple-element.110), channel_id=1, source_target_pairs={{0,1},{1,0},{2,3},{3,2},{4,5},{5,4},{6,7},{7,6},{8,9},{9,8},{10,11... | collective-permute-start | bytes 1572872 | tf_op jit(solution)/shard_map/ppermute | solution.py:312
  54.3 4.3 %collective-permute-done.7.ghost = f32[2,128,256]{2,1,0:T(8,128)S(1)} collective-permute-done((f32[2,128,256]{2,1,0:T(8,128)S(1)}, f32[2,128,256]{2,1,0:T(8,128)S(1)}, u32[]{:S(2)}, u32[]{:S(2)}) %collective-permute-start.7) | collective-permute-done | bytes 262176 | tf_op jit(solution)/shard_map/ppermute | solution.py:309
  61.8 5.9 %shard_map.97 = (f32[2,16,128,256]{3,2,1,0:T(8,128)S(1)}, f32[4,128,256]{2,1,0:T(8,128)S(1)}, f32[16,128,256]{2,1,0:T(8,128)S(1)}, f32[16,128,256]{2,1,0:T(8,128)S(1)}) custom-call(bf16[256,256]{1,0:T(8,128)(2,1)S(1)} %get-tuple-element.77.refs_0_.along_z, ...), custom_call_target="tpu_custom_call", output_to_operand_aliasing={{2}: (11, {}), {3}: (12, {})} | custom-call | flops 1073741824 | bytes 33554432 | tf_op jit(solution)/shard_map/pallas_call | solution.py:342
  67.8 5.2 %collective-permute-start.14 = (f32[4,128,256]{2,1,0:T(8,128)S(1)}, f32[4,128,256]{2,1,0:T(8,128)S(1)}, u32[]{:S(2)}, u32[]{:S(2)}) collective-permute-start(f32[4,128,256]{2,1,0:T(8,128)S(1)} %get-tuple-element.118), channel_id=1, source_target_pairs={{0,1},{1,0},{2,3},{3,2},{4,5},{5,4},{6,7},{7,6},{8,9},{9,8},{10,11... | collective-permute-start | bytes 1572872 | tf_op jit(solution)/shard_map/ppermute | solution.py:312
  74.9 4.3 %collective-permute-done.10.ghost = f32[2,128,256]{2,1,0:T(8,128)S(1)} collective-permute-done((f32[2,128,256]{2,1,0:T(8,128)S(1)}, f32[2,128,256]{2,1,0:T(8,128)S(1)}, u32[]{:S(2)}, u32[]{:S(2)}) %collective-permute-start.10) | collective-permute-done | bytes 262176 | tf_op jit(solution)/shard_map/ppermute | solution.py:309
  82.4 6.1 %shard_map.100 = (f32[2,16,128,256]{3,2,1,0:T(8,128)S(1)}, f32[4,128,256]{2,1,0:T(8,128)S(1)}, f32[16,128,256]{2,1,0:T(8,128)S(1)}, f32[16,128,256]{2,1,0:T(8,128)S(1)}) custom-call(bf16[256,256]{1,0:T(8,128)(2,1)S(1)} %get-tuple-element.77.refs_0_.along_z, ...), custom_call_target="tpu_custom_call", output_to_operand_aliasing={{2}: (11, {}), {3}: (12, {})} | custom-call | flops 1073741824 | bytes 33554432 | tf_op jit(solution)/shard_map/pallas_call | solution.py:342
  88.5 5.2 %collective-permute-start.17 = (f32[4,128,256]{2,1,0:T(8,128)S(1)}, f32[4,128,256]{2,1,0:T(8,128)S(1)}, u32[]{:S(2)}, u32[]{:S(2)}) collective-permute-start(f32[4,128,256]{2,1,0:T(8,128)S(1)} %get-tuple-element.126), channel_id=1, source_target_pairs={{0,1},{1,0},{2,3},{3,2},{4,5},{5,4},{6,7},{7,6},{8,9},{9,8},{10,11... | collective-permute-start | bytes 1572872 | tf_op jit(solution)/shard_map/ppermute | solution.py:312
  95.7 4.3 %collective-permute-done.13.ghost = f32[2,128,256]{2,1,0:T(8,128)S(1)} collective-permute-done((f32[2,128,256]{2,1,0:T(8,128)S(1)}, f32[2,128,256]{2,1,0:T(8,128)S(1)}, u32[]{:S(2)}, u32[]{:S(2)}) %collective-permute-start.13) | collective-permute-done | bytes 262176 | tf_op jit(solution)/shard_map/ppermute | solution.py:309
  103.2 5.9 %shard_map.103 = (f32[2,16,128,256]{3,2,1,0:T(8,128)S(1)}, f32[4,128,256]{2,1,0:T(8,128)S(1)}, f32[16,128,256]{2,1,0:T(8,128)S(1)}, f32[16,128,256]{2,1,0:T(8,128)S(1)}) custom-call(bf16[256,256]{1,0:T(8,128)(2,1)S(1)} %get-tuple-element.77.refs_0_.along_z, ...), custom_call_target="tpu_custom_call", output_to_operand_aliasing={{2}: (11, {}), {3}: (12, {})} | custom-call | flops 1073741824 | bytes 33554432 | tf_op jit(solution)/shard_map/pallas_call | solution.py:342
  109.1 5.2 %collective-permute-start.20 = (f32[4,128,256]{2,1,0:T(8,128)S(1)}, f32[4,128,256]{2,1,0:T(8,128)S(1)}, u32[]{:S(2)}, u32[]{:S(2)}) collective-permute-start(f32[4,128,256]{2,1,0:T(8,128)S(1)} %get-tuple-element.134), channel_id=1, source_target_pairs={{0,1},{1,0},{2,3},{3,2},{4,5},{5,4},{6,7},{7,6},{8,9},{9,8},{10,11... | collective-permute-start | bytes 1572872 | tf_op jit(solution)/shard_map/ppermute | solution.py:312
  116.3 4.3 %collective-permute-done.16.ghost = f32[2,128,256]{2,1,0:T(8,128)S(1)} collective-permute-done((f32[2,128,256]{2,1,0:T(8,128)S(1)}, f32[2,128,256]{2,1,0:T(8,128)S(1)}, u32[]{:S(2)}, u32[]{:S(2)}) %collective-permute-start.16) | collective-permute-done | bytes 262176 | tf_op jit(solution)/shard_map/ppermute | solution.py:309
  123.8 5.9 %shard_map.106 = (f32[2,16,128,256]{3,2,1,0:T(8,128)S(1)}, f32[4,128,256]{2,1,0:T(8,128)S(1)}, f32[16,128,256]{2,1,0:T(8,128)S(1)}, f32[16,128,256]{2,1,0:T(8,128)S(1)}) custom-call(bf16[256,256]{1,0:T(8,128)(2,1)S(1)} %get-tuple-element.77.refs_0_.along_z, ...), custom_call_target="tpu_custom_call", output_to_operand_aliasing={{2}: (11, {}), {3}: (12, {})} | custom-call | flops 1073741824 | bytes 33554432 | tf_op jit(solution)/shard_map/pallas_call | solution.py:342
  129.7 5.2 %collective-permute-start.23 = (f32[4,128,256]{2,1,0:T(8,128)S(1)}, f32[4,128,256]{2,1,0:T(8,128)S(1)}, u32[]{:S(2)}, u32[]{:S(2)}) collective-permute-start(f32[4,128,256]{2,1,0:T(8,128)S(1)} %get-tuple-element.142), channel_id=1, source_target_pairs={{0,1},{1,0},{2,3},{3,2},{4,5},{5,4},{6,7},{7,6},{8,9},{9,8},{10,11... | collective-permute-start | bytes 1572872 | tf_op jit(solution)/shard_map/ppermute | solution.py:312
  136.9 4.3 %collective-permute-done.19.ghost = f32[2,128,256]{2,1,0:T(8,128)S(1)} collective-permute-done((f32[2,128,256]{2,1,0:T(8,128)S(1)}, f32[2,128,256]{2,1,0:T(8,128)S(1)}, u32[]{:S(2)}, u32[]{:S(2)}) %collective-permute-start.19) | collective-permute-done | bytes 262176 | tf_op jit(solution)/shard_map/ppermute | solution.py:309
  146.0 7.3 %shard_map.109 = (f32[2,16,128,256]{3,2,1,0:T(8,128)S(1)}, f32[8,256]{1,0:T(8,128)S(1)}, f32[16,128,256]{2,1,0:T(8,128)S(1)}, f32[16,128,256]{2,1,0:T(8,128)S(1)}) custom-call(bf16[256,256]{1,0:T(8,128)(2,1)S(1)} %get-tuple-element.77.refs_0_.along_z, ...), custom_call_target="tpu_custom_call", output_to_operand_aliasing={{2}: (11, {}), {3}: (12, {})} | custom-call | flops 1073741824 | bytes 33554432 | tf_op jit(solution)/shard_map/pallas_call | solution.py:342
  154.2 11.8 %collective-permute-start.24 = (f32[8,256]{1,0:T(8,128)S(1)}, f32[8,256]{1,0:T(8,128)S(1)}, u32[]{:S(2)}, u32[]{:S(2)}) collective-permute-start(f32[8,256]{1,0:T(8,128)S(1)} %get-tuple-element.151), channel_id=1, source_target_pairs={{0,1},{1,0},{2,3},{3,2},{4,5},{5,4},{6,7},{7,6},{8,9},{9,8},{10,11... | collective-permute-start | bytes 24584 | tf_op jit(solution)/shard_map/ppermute | solution.py:367
  167.1 3.4 %collective-permute-done.25 = f32[8,256]{1,0:T(8,128)S(1)} collective-permute-done((f32[8,256]{1,0:T(8,128)S(1)}, f32[8,256]{1,0:T(8,128)S(1)}, u32[]{:S(2)}, u32[]{:S(2)}) %collective-permute-start.25) | collective-permute-done | bytes 8224 | tf_op jit(solution)/shard_map/ppermute | solution.py:367
  174.2 2.6 %collective-permute-start.27 = (f32[8,256]{1,0:T(8,128)S(1)}, f32[8,256]{1,0:T(8,128)S(1)}, u32[]{:S(2)}, u32[]{:S(2)}) collective-permute-start(f32[8,256]{1,0:T(8,128)S(1)} %max.14), channel_id=1, source_target_pairs={{0,8},{1,9},{2,10},{3,11},{4,12},{5,13},{6,14},{7,15},{8,0},{9,1},... | collective-permute-start | bytes 24584 | tf_op jit(solution)/shard_map/ppermute | solution.py:367
  (72 shorter events, 51.3 us)
Async XLA Ops:
  10.7 10.5 %collective-permute-start.5 = (f32[4,128,256]{2,1,0:T(8,128)S(1)}, f32[4,128,256]{2,1,0:T(8,128)S(1)}, u32[]{:S(2)}, u32[]{:S(2)}) collective-permute-start(f32[4,128,256]{2,1,0:T(8,128)S(1)} %get-tuple-element.94), channel_id=1, source_target_pairs={{0,1},{1,0},{2,3},{3,2},{4,5},{5,4},{6,7},{7,6},{8,9},{9,8},{10,11... | collective-permute-start | bytes 1572872 | tf_op jit(solution)/shard_map/ppermute | solution.py:312
  11.2 7.0 %collective-permute-start.2 = (f32[2,128,256]{2,1,0:T(8,128)S(1)}, f32[2,128,256]{2,1,0:T(8,128)S(1)}, u32[]{:S(2)}, u32[]{:S(2)}) collective-permute-start(f32[2,128,256]{2,1,0:T(8,128)S(1)} %get-tuple-element.88), channel_id=1, source_target_pairs={{0,16},{1,2},{2,1},{3,4},{4,3},{5,6},{6,5},{7,8},{8,7},{9,10},{10,... | collective-permute-start | bytes 786440 | tf_op jit(solution)/shard_map/ppermute | solution.py:309
  13.8 7.2 %collective-permute-start = (f32[2,128,256]{2,1,0:T(8,128)S(1)}, f32[2,128,256]{2,1,0:T(8,128)S(1)}, u32[]{:S(2)}, u32[]{:S(2)}) collective-permute-start(f32[2,128,256]{2,1,0:T(8,128)S(1)} %get-tuple-element.81), channel_id=1, source_target_pairs={{0,16},{1,2},{2,1},{3,4},{4,3},{5,6},{6,5},{7,8},{8,7},{9,10},{10,... | collective-permute-start | bytes 786440 | tf_op jit(solution)/shard_map/ppermute | solution.py:309
  26.9 14.3 %collective-permute-start.8 = (f32[4,128,256]{2,1,0:T(8,128)S(1)}, f32[4,128,256]{2,1,0:T(8,128)S(1)}, u32[]{:S(2)}, u32[]{:S(2)}) collective-permute-start(f32[4,128,256]{2,1,0:T(8,128)S(1)} %get-tuple-element.102), channel_id=1, source_target_pairs={{0,1},{1,0},{2,3},{3,2},{4,5},{5,4},{6,7},{7,6},{8,9},{9,8},{10,11... | collective-permute-start | bytes 1572872 | tf_op jit(solution)/shard_map/ppermute | solution.py:312
  31.7 6.4 %collective-permute-start.4 = (f32[2,128,256]{2,1,0:T(8,128)S(1)}, f32[2,128,256]{2,1,0:T(8,128)S(1)}, u32[]{:S(2)}, u32[]{:S(2)}) collective-permute-start(f32[2,128,256]{2,1,0:T(8,128)S(1)} %get-tuple-element.93), channel_id=1, source_target_pairs={{0,16},{1,2},{2,1},{3,4},{4,3},{5,6},{6,5},{7,8},{8,7},{9,10},{10,... | collective-permute-start | bytes 786440 | tf_op jit(solution)/shard_map/ppermute | solution.py:309
  33.2 7.7 %collective-permute-start.3 = (f32[2,128,256]{2,1,0:T(8,128)S(1)}, f32[2,128,256]{2,1,0:T(8,128)S(1)}, u32[]{:S(2)}, u32[]{:S(2)}) collective-permute-start(f32[2,128,256]{2,1,0:T(8,128)S(1)} %get-tuple-element.91), channel_id=1, source_target_pairs={{0,16},{1,2},{2,1},{3,4},{4,3},{5,6},{6,5},{7,8},{8,7},{9,10},{10,... | collective-permute-start | bytes 786440 | tf_op jit(solution)/shard_map/ppermute | solution.py:309
  47.1 14.7 %collective-permute-start.11 = (f32[4,128,256]{2,1,0:T(8,128)S(1)}, f32[4,128,256]{2,1,0:T(8,128)S(1)}, u32[]{:S(2)}, u32[]{:S(2)}) collective-permute-start(f32[4,128,256]{2,1,0:T(8,128)S(1)} %get-tuple-element.110), channel_id=1, source_target_pairs={{0,1},{1,0},{2,3},{3,2},{4,5},{5,4},{6,7},{7,6},{8,9},{9,8},{10,11... | collective-permute-start | bytes 1572872 | tf_op jit(solution)/shard_map/ppermute | solution.py:312
  52.3 6.4 %collective-permute-start.7 = (f32[2,128,256]{2,1,0:T(8,128)S(1)}, f32[2,128,256]{2,1,0:T(8,128)S(1)}, u32[]{:S(2)}, u32[]{:S(2)}) collective-permute-start(f32[2,128,256]{2,1,0:T(8,128)S(1)} %get-tuple-element.101), channel_id=1, source_target_pairs={{0,16},{1,2},{2,1},{3,4},{4,3},{5,6},{6,5},{7,8},{8,7},{9,10},{10,... | collective-permute-start | bytes 786440 | tf_op jit(solution)/shard_map/ppermute | solution.py:309
  53.8 7.7 %collective-permute-start.6 = (f32[2,128,256]{2,1,0:T(8,128)S(1)}, f32[2,128,256]{2,1,0:T(8,128)S(1)}, u32[]{:S(2)}, u32[]{:S(2)}) collective-permute-start(f32[2,128,256]{2,1,0:T(8,128)S(1)} %get-tuple-element.99), channel_id=1, source_target_pairs={{0,16},{1,2},{2,1},{3,4},{4,3},{5,6},{6,5},{7,8},{8,7},{9,10},{10,... | collective-permute-start | bytes 786440 | tf_op jit(solution)/shard_map/ppermute | solution.py:309
  67.8 14.6 %collective-permute-start.14 = (f32[4,128,256]{2,1,0:T(8,128)S(1)}, f32[4,128,256]{2,1,0:T(8,128)S(1)}, u32[]{:S(2)}, u32[]{:S(2)}) collective-permute-start(f32[4,128,256]{2,1,0:T(8,128)S(1)} %get-tuple-element.118), channel_id=1, source_target_pairs={{0,1},{1,0},{2,3},{3,2},{4,5},{5,4},{6,7},{7,6},{8,9},{9,8},{10,11... | collective-permute-start | bytes 1572872 | tf_op jit(solution)/shard_map/ppermute | solution.py:312
  72.9 6.4 %collective-permute-start.10 = (f32[2,128,256]{2,1,0:T(8,128)S(1)}, f32[2,128,256]{2,1,0:T(8,128)S(1)}, u32[]{:S(2)}, u32[]{:S(2)}) collective-permute-start(f32[2,128,256]{2,1,0:T(8,128)S(1)} %get-tuple-element.109), channel_id=1, source_target_pairs={{0,16},{1,2},{2,1},{3,4},{4,3},{5,6},{6,5},{7,8},{8,7},{9,10},{10,... | collective-permute-start | bytes 786440 | tf_op jit(solution)/shard_map/ppermute | solution.py:309
  74.4 7.7 %collective-permute-start.9 = (f32[2,128,256]{2,1,0:T(8,128)S(1)}, f32[2,128,256]{2,1,0:T(8,128)S(1)}, u32[]{:S(2)}, u32[]{:S(2)}) collective-permute-start(f32[2,128,256]{2,1,0:T(8,128)S(1)} %get-tuple-element.107), channel_id=1, source_target_pairs={{0,16},{1,2},{2,1},{3,4},{4,3},{5,6},{6,5},{7,8},{8,7},{9,10},{10,... | collective-permute-start | bytes 786440 | tf_op jit(solution)/shard_map/ppermute | solution.py:309
  88.5 14.7 %collective-permute-start.17 = (f32[4,128,256]{2,1,0:T(8,128)S(1)}, f32[4,128,256]{2,1,0:T(8,128)S(1)}, u32[]{:S(2)}, u32[]{:S(2)}) collective-permute-start(f32[4,128,256]{2,1,0:T(8,128)S(1)} %get-tuple-element.126), channel_id=1, source_target_pairs={{0,1},{1,0},{2,3},{3,2},{4,5},{5,4},{6,7},{7,6},{8,9},{9,8},{10,11... | collective-permute-start | bytes 1572872 | tf_op jit(solution)/shard_map/ppermute | solution.py:312
  93.7 6.4 %collective-permute-start.13 = (f32[2,128,256]{2,1,0:T(8,128)S(1)}, f32[2,128,256]{2,1,0:T(8,128)S(1)}, u32[]{:S(2)}, u32[]{:S(2)}) collective-permute-start(f32[2,128,256]{2,1,0:T(8,128)S(1)} %get-tuple-element.117), channel_id=1, source_target_pairs={{0,16},{1,2},{2,1},{3,4},{4,3},{5,6},{6,5},{7,8},{8,7},{9,10},{10,... | collective-permute-start | bytes 786440 | tf_op jit(solution)/shard_map/ppermute | solution.py:309
  95.2 7.7 %collective-permute-start.12 = (f32[2,128,256]{2,1,0:T(8,128)S(1)}, f32[2,128,256]{2,1,0:T(8,128)S(1)}, u32[]{:S(2)}, u32[]{:S(2)}) collective-permute-start(f32[2,128,256]{2,1,0:T(8,128)S(1)} %get-tuple-element.115), channel_id=1, source_target_pairs={{0,16},{1,2},{2,1},{3,4},{4,3},{5,6},{6,5},{7,8},{8,7},{9,10},{10,... | collective-permute-start | bytes 786440 | tf_op jit(solution)/shard_map/ppermute | solution.py:309
  109.1 14.7 %collective-permute-start.20 = (f32[4,128,256]{2,1,0:T(8,128)S(1)}, f32[4,128,256]{2,1,0:T(8,128)S(1)}, u32[]{:S(2)}, u32[]{:S(2)}) collective-permute-start(f32[4,128,256]{2,1,0:T(8,128)S(1)} %get-tuple-element.134), channel_id=1, source_target_pairs={{0,1},{1,0},{2,3},{3,2},{4,5},{5,4},{6,7},{7,6},{8,9},{9,8},{10,11... | collective-permute-start | bytes 1572872 | tf_op jit(solution)/shard_map/ppermute | solution.py:312
  114.3 6.4 %collective-permute-start.16 = (f32[2,128,256]{2,1,0:T(8,128)S(1)}, f32[2,128,256]{2,1,0:T(8,128)S(1)}, u32[]{:S(2)}, u32[]{:S(2)}) collective-permute-start(f32[2,128,256]{2,1,0:T(8,128)S(1)} %get-tuple-element.125), channel_id=1, source_target_pairs={{0,16},{1,2},{2,1},{3,4},{4,3},{5,6},{6,5},{7,8},{8,7},{9,10},{10,... | collective-permute-start | bytes 786440 | tf_op jit(solution)/shard_map/ppermute | solution.py:309
  115.8 7.7 %collective-permute-start.15 = (f32[2,128,256]{2,1,0:T(8,128)S(1)}, f32[2,128,256]{2,1,0:T(8,128)S(1)}, u32[]{:S(2)}, u32[]{:S(2)}) collective-permute-start(f32[2,128,256]{2,1,0:T(8,128)S(1)} %get-tuple-element.123), channel_id=1, source_target_pairs={{0,16},{1,2},{2,1},{3,4},{4,3},{5,6},{6,5},{7,8},{8,7},{9,10},{10,... | collective-permute-start | bytes 786440 | tf_op jit(solution)/shard_map/ppermute | solution.py:309
  129.7 16.3 %collective-permute-start.23 = (f32[4,128,256]{2,1,0:T(8,128)S(1)}, f32[4,128,256]{2,1,0:T(8,128)S(1)}, u32[]{:S(2)}, u32[]{:S(2)}) collective-permute-start(f32[4,128,256]{2,1,0:T(8,128)S(1)} %get-tuple-element.142), channel_id=1, source_target_pairs={{0,1},{1,0},{2,3},{3,2},{4,5},{5,4},{6,7},{7,6},{8,9},{9,8},{10,11... | collective-permute-start | bytes 1572872 | tf_op jit(solution)/shard_map/ppermute | solution.py:312
  134.9 6.4 %collective-permute-start.19 = (f32[2,128,256]{2,1,0:T(8,128)S(1)}, f32[2,128,256]{2,1,0:T(8,128)S(1)}, u32[]{:S(2)}, u32[]{:S(2)}) collective-permute-start(f32[2,128,256]{2,1,0:T(8,128)S(1)} %get-tuple-element.133), channel_id=1, source_target_pairs={{0,16},{1,2},{2,1},{3,4},{4,3},{5,6},{6,5},{7,8},{8,7},{9,10},{10,... | collective-permute-start | bytes 786440 | tf_op jit(solution)/shard_map/ppermute | solution.py:309
  136.4 7.7 %collective-permute-start.18 = (f32[2,128,256]{2,1,0:T(8,128)S(1)}, f32[2,128,256]{2,1,0:T(8,128)S(1)}, u32[]{:S(2)}, u32[]{:S(2)}) collective-permute-start(f32[2,128,256]{2,1,0:T(8,128)S(1)} %get-tuple-element.131), channel_id=1, source_target_pairs={{0,16},{1,2},{2,1},{3,4},{4,3},{5,6},{6,5},{7,8},{8,7},{9,10},{10,... | collective-permute-start | bytes 786440 | tf_op jit(solution)/shard_map/ppermute | solution.py:309
  141.6 11.7 %collective-permute-start.22 = (f32[2,128,256]{2,1,0:T(8,128)S(1)}, f32[2,128,256]{2,1,0:T(8,128)S(1)}, u32[]{:S(2)}, u32[]{:S(2)}) collective-permute-start(f32[2,128,256]{2,1,0:T(8,128)S(1)} %get-tuple-element.141), channel_id=1, source_target_pairs={{0,16},{1,2},{2,1},{3,4},{4,3},{5,6},{6,5},{7,8},{8,7},{9,10},{10,... | collective-permute-start | bytes 786440 | tf_op jit(solution)/shard_map/ppermute | solution.py:309
  144.4 9.2 %collective-permute-start.21 = (f32[2,128,256]{2,1,0:T(8,128)S(1)}, f32[2,128,256]{2,1,0:T(8,128)S(1)}, u32[]{:S(2)}, u32[]{:S(2)}) collective-permute-start(f32[2,128,256]{2,1,0:T(8,128)S(1)} %get-tuple-element.139), channel_id=1, source_target_pairs={{0,16},{1,2},{2,1},{3,4},{4,3},{5,6},{6,5},{7,8},{8,7},{9,10},{10,... | collective-permute-start | bytes 786440 | tf_op jit(solution)/shard_map/ppermute | solution.py:309
  154.2 12.6 %collective-permute-start.24 = (f32[8,256]{1,0:T(8,128)S(1)}, f32[8,256]{1,0:T(8,128)S(1)}, u32[]{:S(2)}, u32[]{:S(2)}) collective-permute-start(f32[8,256]{1,0:T(8,128)S(1)} %get-tuple-element.151), channel_id=1, source_target_pairs={{0,1},{1,0},{2,3},{3,2},{4,5},{5,4},{6,7},{7,6},{8,9},{9,8},{10,11... | collective-permute-start | bytes 24584 | tf_op jit(solution)/shard_map/ppermute | solution.py:367
  (7 other events, 20.1 us)
